TPU v7x, 32 devices: a whole 2x2x4 slice. The times are simulated.
32 devices in a mesh: batch: 2 (over y), region: 4 (over z), scen: 2 (over x), row: 2 (over core).
Axes of the slice: x: 2, y: 2, z: 4, core: 2. Of those that a mesh axis runs over, the one named last changes fastest.
Arguments:
- kkt_inverse: bfloat16 [4, 1536, 1536], P('region', 'row'), may hold values from -0.25 to 1.25, as said below
- bus_load: bfloat16 [4, 1536, 1024], P('region', None, ('batch', 'scen', 'row')), parts along dimension 2, may hold values from -6 to 6
- bus_limit: float32 [4, 1536], P('region'), may hold values from 0.3 to 3
- copy_local: int32 [4, 128], P('region'), may hold values from 0 to 1535, as said below
- copy_dest: int32 [4, 128], P('region'), may hold values from 0 to 3, as said below
- copy_slot: int32 [4, 128], P('region'), may hold values from 0 to 63, as said below
- copy_key: int32 [4, 128], P('region'), may hold values from 0 to 63
- own_key: int32 [4, 4, 64], P('region'), may hold values from -1 to 63, as said below
Outputs:
- dispatch: float32 [4, 1536, 1024], P('region', None, ('batch', 'scen', 'row')), parts along dimension 2
- scaled_duals: float32 [4, 128, 1024], P('region', None, ('batch', 'scen', 'row')), parts along dimension 2
There are 2 independent parts, one for each index of `batch`. A program takes and returns all parts, laid end to end along the dimension named above; an argument that names none is the same for every part. Nothing has to cross between parts.
Inputs may be any that keep to these rules, and one draw needn't show every extreme that they name: `copy_local`: the 128 local buses of one region's copies are distinct. `copy_dest`: A region sends at most 64 copies to one owner; in every draw one owner receives exactly 64 copies from every region. `copy_slot`: within one region, copies with the same owner have distinct slots. own_key[o, r, s] equals copy_key[r, k] for the copy k of region r with copy_dest o and copy_slot s, and -1 where region r has no such copy. `kkt_inverse`: each matrix has a diagonal of 0.75 to 1.25 and independent off-diagonal entries.
All inputs are finite; a program needn't handle non-finite values.
Results may differ from a plain program's by a relative error of at most 0.0026.
Values may be sent and summed in bfloat16 or wider, within the bound.
No kernel may reach another device: no remote copies, remote signals or barrier semaphores. Data moves between devices by JAX's collectives and lax.ppermute only.
A program may use at most 64 MiB of HBM per device.

v0:
```python
import jax
import jax.numpy as jnp
from jax import lax
from jax.sharding import PartitionSpec as P

GO = 64
ITERS = 3


PENALTY = 1.0
PROXIMAL = 0.5


def per_device(
    kkt_inverse, bus_load, bus_limit, copy_local, copy_dest, copy_slot, copy_key, own_key
):
    inverse_rows = kkt_inverse[0]
    load_cols = bus_load[0].astype(jnp.float32)
    limit_all = bus_limit[0]
    local_rows = copy_local[0]
    dest_rows = copy_dest[0]
    slot_rows = copy_slot[0]
    owner_keys = own_key[0].reshape(-1)
    regions = lax.axis_size("region")
    capacity = own_key.shape[2]
    bus_count = load_cols.shape[0]
    column_count = load_cols.shape[1]
    copy_count = local_rows.shape[0]
    send_rows = dest_rows * capacity + slot_rows
    selector = (owner_keys[None, :] == jnp.arange(GO, dtype=jnp.int32)[:, None]).astype(jnp.float32)
    tallies = jnp.maximum(jnp.sum(selector, axis=1), 1.0)
    fetch_rows = jnp.where(owner_keys >= 0, owner_keys, 0)
    dispatch = jnp.zeros((bus_count, column_count), jnp.float32)
    dual_vals = jnp.zeros((copy_count, column_count), jnp.float32)
    consensus = jnp.zeros((copy_count, column_count), jnp.float32)
    for iteration in range(ITERS):
        boundary = (
            jnp.zeros((bus_count, column_count), jnp.float32)
            .at[local_rows]
            .add(consensus - dual_vals)
        )
        drive_cols = (load_cols + PROXIMAL * dispatch + PENALTY * boundary).astype(jnp.bfloat16)
        half_rows = inverse_rows.shape[0]
        first_row = lax.axis_index("row") * half_rows
        limit_half = lax.dynamic_slice_in_dim(limit_all, first_row, half_rows, 0)
        solved = jnp.dot(
            inverse_rows,
            lax.all_gather(drive_cols, "row", axis=1, tiled=True),
            preferred_element_type=jnp.float32,
        )
        clipped = jnp.clip(solved, -limit_half[:, None], limit_half[:, None])
        dispatch = lax.all_to_all(clipped, "row", split_axis=1, concat_axis=0, tiled=True)
        at_copies = dispatch[local_rows]
        shared = at_copies + dual_vals
        packed = (
            jnp.zeros((regions * capacity, column_count), jnp.float32).at[send_rows].set(shared)
        )
        packed = packed.reshape(regions, capacity, column_count)
        arrived = lax.all_to_all(packed, "region", split_axis=0, concat_axis=0, tiled=True)
        totals = jnp.dot(
            selector,
            arrived.reshape(-1, column_count),
            precision=lax.Precision.HIGHEST,
            preferred_element_type=jnp.float32,
        )
        averages = totals / tallies[:, None]
        replies = averages[fetch_rows].reshape(regions, capacity, column_count)
        answered = lax.all_to_all(replies, "region", split_axis=0, concat_axis=0, tiled=True)
        consensus = answered.reshape(-1, column_count)[send_rows]
        dual_vals = dual_vals + at_copies - consensus
    return (dispatch[None], dual_vals[None])


def solution(mesh):
    return jax.shard_map(
        per_device,
        mesh=mesh,
        in_specs=(
            P("region", "row", None),
            P("region", None, ("batch", "scen", "row")),
            P("region", None),
            P("region", None),
            P("region", None),
            P("region", None),
            P("region", None),
            P("region", None, None),
        ),
        out_specs=(
            P("region", None, ("batch", "scen", "row")),
            P("region", None, ("batch", "scen", "row")),
        ),
        check_vma=False,
    )
```

profile of v0, /device:TPU:0, one launch (start us, length us, event | category | flops | bytes accessed | tf_op | source)
XLA Modules:
  0.0 114.3 jit_solution(6413281735627667836)
XLA Ops:
  0.6 0.8 fusion.39
  1.5 0.7 dynamic-slice_reduce_fusion
  2.2 1.1 bitcast_convert_fusion
  3.2 1.6 %scatter_custom_fusion = f32[1536,128]{1,0:T(8,128)S(1)} fusion(f32[1536,128]{1,0:T(8,128)S(1)} %bitcast_convert_fusion, s32[128]{0:T(128)S(1)} %fusion.39, f32[]{:T(128)} %constant.13.clone.1), kind=kCustom, calls=%fused_computation.46 | custom fusion | flops 16384 | bytes 786436 | tf_op jit(solution)/shard_map/scatter-add | solution.py:40
  4.8 2.5 %all_gather.9 = bf16[1536,256]{1,0:T(8,128)(2,1)S(1)} all-gather(bf16[1536,128]{1,0:T(8,128)(2,1)S(1)} %convert_element_type.20), channel_id=1, replica_groups=mesh['batch'=2,'region'=4,'scen'=2,'row'=2] {'row'}, dimensions={1}, use_global_device_ids=true | all-gather | bytes 1179648 | tf_op jit(solution)/shard_map/all_gather | solution.py:48
  7.4 1.7 %fusion.9 = f32[256,768]{1,0:T(8,128)} fusion(bf16[1536,256]{1,0:T(8,128)(2,1)S(1)} %all_gather.9, bf16[1,768,1536]{2,1,0:T(8,128)(2,1)S(1)} %copy-done, f32[768]{0:T(1024)S(1)} %neg.10, f32[768]{0:T(1024)S(1)} %dynamic-slice_reduce_fusion), kind=kOutput, calls=%fused_computation.22 | convolution fusion | flops 604372992 | bytes 3938304 | tf_op jit(solution)/shard_map/dot_general | solution.py:46
  9.1 3.7 %all-to-all-start = ((f32[768,2,128]{0,2,1:T(8,128)}), f32[768,2,128]{0,2,1:T(8,128)S(1)}, u32[]{:S(2)}, u32[]{:S(2)}) async-start(f32[768,2,128]{0,2,1:T(8,128)} %bitcast.84), calls=%async_computation | async-start | bytes 1572864 | tf_op jit(solution)/shard_map/all_to_all | solution.py:52
  12.8 1.9 %all-to-all-done = f32[768,2,128]{0,2,1:T(8,128)S(1)} async-done(((f32[768,2,128]{0,2,1:T(8,128)}), f32[768,2,128]{0,2,1:T(8,128)S(1)}, u32[]{:S(2)}, u32[]{:S(2)}) %all-to-all-start) | async-done | bytes 786464 | tf_op jit(solution)/shard_map/all_to_all | solution.py:52
  14.7 0.9 copy-done.1
  15.5 1.4 %copy.13 = f32[2,768,128]{2,1,0:T(8,128)S(1)} copy(f32[2,768,128]{1,2,0:T(8,128)} %bitcast.79) | data formatting | bytes 1572864 | tf_op jit(solution)/shard_map/all_to_all | solution.py:52
  17.0 0.6 gather_fusion
  17.6 1.5 %scatter_custom_fusion.1 = f32[256,128]{1,0:T(8,128)} fusion(s32[128]{0:T(128)S(1)} %fusion.40, f32[128,128]{1,0:T(8,128)S(1)} %gather_fusion, f32[]{:T(128)} %constant.13.clone.1), kind=kCustom, calls=%fused_computation.43 | custom fusion | bytes 131076 | tf_op jit(solution)/shard_map/scatter | solution.py:56
  19.1 6.2 %all-to-all-start.1 = ((f32[4,64,128]{2,1,0:T(8,128)}), f32[4,64,128]{2,1,0:T(8,128)S(1)}, u32[]{:S(2)}, u32[]{:S(2)}) async-start(f32[4,64,128]{2,1,0:T(8,128)} %bitcast.11), calls=%async_computation.1 | async-start | bytes 262144 | tf_op jit(solution)/shard_map/all_to_all | solution.py:59
  25.6 5.9 %all-to-all-done.1 = f32[4,64,128]{2,1,0:T(8,128)S(1)} async-done(((f32[4,64,128]{2,1,0:T(8,128)}), f32[4,64,128]{2,1,0:T(8,128)S(1)}, u32[]{:S(2)}, u32[]{:S(2)}) %all-to-all-start.1) | async-done | bytes 131104 | tf_op jit(solution)/shard_map/all_to_all | solution.py:59
  31.5 0.2 convolution_divide_fusion.2
  31.7 1.3 %gather_fusion.1 = f32[256,128]{1,0:T(8,128)} fusion(f32[64,128]{1,0:T(8,128)S(1)} %convolution_divide_fusion.2, s32[1024]{0:T(1024)S(1)} %pad_clamp_fusion.1), kind=kCustom, calls=%fused_computation.1 | custom fusion | bytes 263168 | tf_op jit(solution)/shard_map/gather | solution.py:67
  33.1 3.3 %all-to-all-start.2 = ((f32[4,64,128]{2,1,0:T(8,128)}), f32[4,64,128]{2,1,0:T(8,128)S(1)}, u32[]{:S(2)}, u32[]{:S(2)}) async-start(f32[4,64,128]{2,1,0:T(8,128)} %bitcast.14), calls=%async_computation.2 | async-start | bytes 262144 | tf_op jit(solution)/shard_map/all_to_all | solution.py:68
  36.4 2.0 %multiply_add_fusion.1 = f32[1536,128]{1,0:T(8,128)} fusion(bf16[1,1536,128]{2,1,0:T(8,128)(2,1)} %param.9, f32[2,768,128]{2,1,0:T(8,128)S(1)} %copy.13), kind=kLoop, calls=%fused_computation.31 | loop fusion | flops 589824 | bytes 1966080 | tf_op jit(solution)/shard_map/add | solution.py:42
  38.3 3.9 %all-to-all-done.2 = f32[4,64,128]{2,1,0:T(8,128)S(1)} async-done(((f32[4,64,128]{2,1,0:T(8,128)}), f32[4,64,128]{2,1,0:T(8,128)S(1)}, u32[]{:S(2)}, u32[]{:S(2)}) %all-to-all-start.2) | async-done | bytes 131104 | tf_op jit(solution)/shard_map/all_to_all | solution.py:68
  42.3 0.6 gather_fusion.2
  42.9 3.2 %scatter_custom_fusion.2 = f32[1536,128]{1,0:T(8,128)} fusion(f32[1536,128]{1,0:T(8,128)} %multiply_add_fusion.1, s32[128]{0:T(128)S(1)} %fusion.39, f32[128,128]{1,0:T(8,128)S(1)} %gather_fusion.2, f32[128,128]{1,0:T(8,128)S(1)} %sub.42), kind=kCustom, calls=%fused_computation.36 | custom fusion | flops 32768 | bytes 917504 | tf_op jit(solution)/shard_map/scatter-add | solution.py:40
  46.1 1.2 %convert_element_type.22 = bf16[1536,128]{1,0:T(8,128)(2,1)S(1)} convert(f32[1536,128]{1,0:T(8,128)} %scatter_custom_fusion.2) | non-fusion elementwise | flops 196608 | bytes 1179648 | tf_op jit(solution)/shard_map/convert_element_type | solution.py:42
  47.3 2.4 %all_gather.10 = bf16[1536,256]{1,0:T(8,128)(2,1)S(1)} all-gather(bf16[1536,128]{1,0:T(8,128)(2,1)S(1)} %convert_element_type.22), channel_id=1, replica_groups=mesh['batch'=2,'region'=4,'scen'=2,'row'=2] {'row'}, dimensions={1}, use_global_device_ids=true | all-gather | bytes 1179648 | tf_op jit(solution)/shard_map/all_gather | solution.py:48
  49.7 0.8 fusion.15
  50.5 5.1 %all_to_all.87 = f32[768,2,128]{0,2,1:T(8,128)} all-to-all(f32[768,2,128]{0,2,1:T(8,128)S(1)} %bitcast.86), channel_id=1, replica_groups=mesh['batch'=2,'region'=4,'scen'=2,'row'=2] {'row'}, dimensions={1} | all-to-all | bytes 1572864 | tf_op jit(solution)/shard_map/all_to_all | solution.py:52
  55.6 1.4 %copy.14 = f32[2,768,128]{2,1,0:T(8,128)S(1)} copy(f32[2,768,128]{1,2,0:T(8,128)} %bitcast.80) | data formatting | bytes 1572864 | tf_op jit(solution)/shard_map/all_to_all | solution.py:52
  57.0 0.7 gather_fusion.3
  57.7 0.9 scatter_custom_fusion.3
  58.6 8.9 %all_to_all.88 = f32[4,64,128]{2,1,0:T(8,128)S(1)} all-to-all(f32[4,64,128]{2,1,0:T(8,128)S(1)} %bitcast.91), channel_id=1, replica_groups=mesh['batch'=2,'region'=4,'scen'=2,'row'=2] {'region'}, dimensions={0} | all-to-all | bytes 262144 | tf_op jit(solution)/shard_map/all_to_all | solution.py:59
  67.5 0.2 convolution_divide_fusion.1
  67.7 1.3 %gather_fusion.4 = f32[256,128]{1,0:T(8,128)} fusion(f32[64,128]{1,0:T(8,128)S(1)} %convolution_divide_fusion.1, s32[1024]{0:T(1024)S(1)} %pad_clamp_fusion.1), kind=kCustom, calls=%fused_computation.4 | custom fusion | bytes 263168 | tf_op jit(solution)/shard_map/gather | solution.py:67
  69.0 3.3 %all-to-all-start.5 = ((f32[4,64,128]{2,1,0:T(8,128)}), f32[4,64,128]{2,1,0:T(8,128)S(1)}, u32[]{:S(2)}, u32[]{:S(2)}) async-start(f32[4,64,128]{2,1,0:T(8,128)} %bitcast.22), calls=%async_computation.5 | async-start | bytes 262144 | tf_op jit(solution)/shard_map/all_to_all | solution.py:68
  72.3 2.0 %multiply_add_fusion = f32[1536,128]{1,0:T(8,128)} fusion(bf16[1,1536,128]{2,1,0:T(8,128)(2,1)} %param.9, f32[2,768,128]{2,1,0:T(8,128)S(1)} %copy.14), kind=kLoop, calls=%fused_computation.30 | loop fusion | flops 589824 | bytes 1966080 | tf_op jit(solution)/shard_map/add | solution.py:42
  74.3 3.9 %all-to-all-done.5 = f32[4,64,128]{2,1,0:T(8,128)S(1)} async-done(((f32[4,64,128]{2,1,0:T(8,128)}), f32[4,64,128]{2,1,0:T(8,128)S(1)}, u32[]{:S(2)}, u32[]{:S(2)}) %all-to-all-start.5) | async-done | bytes 131104 | tf_op jit(solution)/shard_map/all_to_all | solution.py:68
  78.2 0.6 gather_fusion.5
  78.9 3.2 %scatter_custom_fusion.4 = f32[1536,128]{1,0:T(8,128)} fusion(f32[1536,128]{1,0:T(8,128)} %multiply_add_fusion, s32[128]{0:T(128)S(1)} %fusion.39, f32[128,128]{1,0:T(8,128)S(1)} %gather_fusion.5, f32[128,128]{1,0:T(8,128)S(1)} %sub.44), kind=kCustom, calls=%fused_computation.34 | custom fusion | flops 32768 | bytes 917504 | tf_op jit(solution)/shard_map/scatter-add | solution.py:40
  82.0 1.2 %convert_element_type.23 = bf16[1536,128]{1,0:T(8,128)(2,1)S(1)} convert(f32[1536,128]{1,0:T(8,128)} %scatter_custom_fusion.4) | non-fusion elementwise | flops 196608 | bytes 1179648 | tf_op jit(solution)/shard_map/convert_element_type | solution.py:42
  83.2 2.4 %all_gather.11 = bf16[1536,256]{1,0:T(8,128)(2,1)S(1)} all-gather(bf16[1536,128]{1,0:T(8,128)(2,1)S(1)} %convert_element_type.23), channel_id=1, replica_groups=mesh['batch'=2,'region'=4,'scen'=2,'row'=2] {'row'}, dimensions={1}, use_global_device_ids=true | all-gather | bytes 1179648 | tf_op jit(solution)/shard_map/all_gather | solution.py:48
  85.6 0.8 fusion.21
  86.4 4.4 %all_to_all.89 = f32[768,2,128]{0,2,1:T(8,128)S(1)} all-to-all(f32[768,2,128]{0,2,1:T(8,128)S(1)} %bitcast.85), channel_id=1, replica_groups=mesh['batch'=2,'region'=4,'scen'=2,'row'=2] {'row'}, dimensions={1} | all-to-all | bytes 1572864 | tf_op jit(solution)/shard_map/all_to_all | solution.py:52
  90.8 1.1 %copy.15 = f32[2,768,128]{2,1,0:T(8,128)} copy(f32[2,768,128]{1,2,0:T(8,128)S(1)} %bitcast.81) | data formatting | bytes 1572864 | tf_op jit(solution)/shard_map/all_to_all | solution.py:52
  92.0 1.8 %gather_fusion.6 = f32[128,128]{1,0:T(8,128)S(1)} fusion(f32[1536,128]{1,0:T(8,128)} %bitcast.82, s32[1024]{0:T(1024)S(1)} %pad_clamp_fusion.2), kind=kCustom, calls=%fused_computation.6 | custom fusion | bytes 131584 | tf_op jit(solution)/shard_map/gather | solution.py:53
  93.8 0.9 scatter_custom_fusion.5
  94.7 8.9 %all_to_all.90 = f32[4,64,128]{2,1,0:T(8,128)S(1)} all-to-all(f32[4,64,128]{2,1,0:T(8,128)S(1)} %bitcast.90), channel_id=1, replica_groups=mesh['batch'=2,'region'=4,'scen'=2,'row'=2] {'region'}, dimensions={0} | all-to-all | bytes 262144 | tf_op jit(solution)/shard_map/all_to_all | solution.py:59
  103.7 0.7 gather_fusion.7
  104.5 8.6 %all_to_all.91 = f32[4,64,128]{2,1,0:T(8,128)S(1)} all-to-all(f32[4,64,128]{2,1,0:T(8,128)S(1)} %bitcast.92), channel_id=1, replica_groups=mesh['batch'=2,'region'=4,'scen'=2,'row'=2] {'region'}, dimensions={0} | all-to-all | bytes 262144 | tf_op jit(solution)/shard_map/all_to_all | solution.py:68
  113.1 0.6 gather_fusion.8
  113.7 0.6 subtract_bitcast_fusion
  (25 shorter events, 0.6 us)
Async XLA Ops:
  0.6 6.7 %copy-start = (bf16[1,768,1536]{2,1,0:T(8,128)(2,1)S(1)}, bf16[1,768,1536]{2,1,0:T(8,128)(2,1)}, u32[]{:S(2)}) copy-start(bf16[1,768,1536]{2,1,0:T(8,128)(2,1)} %param.8) | copy-start | bytes 7077892
  9.1 7.9 %copy-start.3 = (s32[1,128]{1,0:T(1,128)S(1)}, s32[1,128]{1,0:T(1,128)}, u32[]{:S(2)}) copy-start(s32[1,128]{1,0:T(1,128)} %param.13) | copy-start | bytes 1540
  9.1 7.9 %copy-start.4 = (s32[1,128]{1,0:T(1,128)S(1)}, s32[1,128]{1,0:T(1,128)}, u32[]{:S(2)}) copy-start(s32[1,128]{1,0:T(1,128)} %param.12) | copy-start | bytes 1540
  9.1 16.3 %copy-start.2 = (s32[1,4,64]{2,1,0:T(4,128)S(1)}, s32[1,4,64]{2,1,0:T(4,128)}, u32[]{:S(2)}) copy-start(s32[1,4,64]{2,1,0:T(4,128)} %param.14) | copy-start | bytes 3076
  9.1 5.6 %all-to-all-start = ((f32[768,2,128]{0,2,1:T(8,128)}), f32[768,2,128]{0,2,1:T(8,128)S(1)}, u32[]{:S(2)}, u32[]{:S(2)}) async-start(f32[768,2,128]{0,2,1:T(8,128)} %bitcast.84), calls=%async_computation | async-start | bytes 1572864 | tf_op jit(solution)/shard_map/all_to_all | solution.py:52
  14.7 0.9 copy-start.1
  19.1 12.4 %all-to-all-start.1 = ((f32[4,64,128]{2,1,0:T(8,128)}), f32[4,64,128]{2,1,0:T(8,128)S(1)}, u32[]{:S(2)}, u32[]{:S(2)}) async-start(f32[4,64,128]{2,1,0:T(8,128)} %bitcast.11), calls=%async_computation.1 | async-start | bytes 262144 | tf_op jit(solution)/shard_map/all_to_all | solution.py:59
  33.1 9.2 %all-to-all-start.2 = ((f32[4,64,128]{2,1,0:T(8,128)}), f32[4,64,128]{2,1,0:T(8,128)S(1)}, u32[]{:S(2)}, u32[]{:S(2)}) async-start(f32[4,64,128]{2,1,0:T(8,128)} %bitcast.14), calls=%async_computation.2 | async-start | bytes 262144 | tf_op jit(solution)/shard_map/all_to_all | solution.py:68
  69.0 9.2 %all-to-all-start.5 = ((f32[4,64,128]{2,1,0:T(8,128)}), f32[4,64,128]{2,1,0:T(8,128)S(1)}, u32[]{:S(2)}, u32[]{:S(2)}) async-start(f32[4,64,128]{2,1,0:T(8,128)} %bitcast.22), calls=%async_computation.5 | async-start | bytes 262144 | tf_op jit(solution)/shard_map/all_to_all | solution.py:68
where the time goes:
time: 116 us; the launch traced here: 114 us
  blocking collectives  43.2 us (37%)
  local copies, waits for them, and re-layouts  17.4 us (15%)
  other arithmetic  16.9 us (15%)
  starting transfers between devices  16.5 us (14%)
  waiting for transfers between devices  15.7 us (14%)
  matrix products  3.89 us (3%)
    all_to_all x2, blocking collectives, per_device(): lax.all_to_all(packed, 'region', split_axis=0, concat_axis=0, tiled=True)  17.8 us
    all_to_all x2, blocking collectives, per_device(): lax.all_to_all(clipped, 'row', split_axis=1, concat_axis=0, tiled=True)  9.49 us
    all_to_all x1, blocking collectives, per_device(): lax.all_to_all(replies, 'region', split_axis=0, concat_axis=0, tiled=True)  8.6 us
    scatter-add x3, other arithmetic, per_device(): boundary = jnp.zeros((bus_count, column_count), jnp.float32).at[local_row...  7.89 us
    all_to_all x2, waiting for transfers between devices, per_device(): lax.all_to_all(replies, 'region', split_axis=0, concat_axis=0, tiled=True)  7.86 us
    all_gather x3, blocking collectives, per_device(): lax.all_gather(drive_cols, 'row', axis=1, tiled=True)  7.31 us
    all_to_all x2, starting transfers between devices, per_device(): lax.all_to_all(replies, 'region', split_axis=0, concat_axis=0, tiled=True)  6.65 us
    all_to_all x1, starting transfers between devices, per_device(): lax.all_to_all(packed, 'region', split_axis=0, concat_axis=0, tiled=True)  6.23 us
  transfers between devices with their start and end apart: 4, of which 4 were waited for; matrix products, arithmetic and copies ran while one was open for 4% of the time, Pallas kernels for 0%

commit v1 on v0

v1 whole, which is shorter than its diff:
```python
import jax
import jax.numpy as jnp
from jax import lax
from jax.sharding import PartitionSpec as P

GO = 64
ITERS = 3
PENALTY = 1.0
PROXIMAL = 0.5
F32 = jnp.float32
BF16 = jnp.bfloat16


def dot32(a, b, precision=None):
    return jnp.dot(a, b, precision=precision, preferred_element_type=F32)


def swap_row(x):
    return lax.ppermute(x, "row", [(0, 1), (1, 0)])


def from_others(x, regions):
    if regions & (regions - 1) == 0 and regions <= 8:
        return [
            lax.ppermute(x, "region", [(i, i ^ s) for i in range(regions)])
            for s in range(1, regions)
        ]
    everyone = lax.all_gather(x, "region", axis=0)
    me = lax.axis_index("region")
    return [
        lax.dynamic_index_in_dim(everyone, lax.rem(me + s, regions), 0, keepdims=False)
        for s in range(1, regions)
    ]


def per_device(
    kkt_inverse, bus_load, bus_limit, copy_local, copy_dest, copy_slot, copy_key, own_key
):
    del copy_slot, own_key
    kh = kkt_inverse[0]
    load = bus_load[0]
    limit = bus_limit[0]
    local_rows = copy_local[0]
    dest = copy_dest[0]
    key = copy_key[0]
    regions = lax.axis_size("region")
    half, buses = kh.shape
    cols = load.shape[1]
    copies = local_rows.shape[0]
    h = lax.axis_index("row")
    first = h * half
    other = half - first

    bus_ids = lax.broadcasted_iota(jnp.int32, (copies, buses), 1)
    picked = local_rows[:, None] == bus_ids
    pick = picked.astype(BF16)
    place = (
        lax.broadcasted_iota(jnp.int32, (buses, copies), 0) == local_rows[None, :]
    ).astype(BF16)
    pick_half = (
        local_rows[:, None] - first == lax.broadcasted_iota(jnp.int32, (copies, half), 1)
    ).astype(BF16)
    keep = 1.0 - jnp.sum(place.astype(F32), axis=1, keepdims=True)

    kc_part = dot32(pick_half, kh).astype(BF16)
    kc_other = swap_row(kc_part)
    ko = swap_row(kh)
    kc = kc_part + kc_other
    load_c = dot32(pick, load)
    limit_c = jnp.sum(jnp.where(picked, limit[None, :], 0.0), axis=1, keepdims=True)
    kcc = dot32(kc, place).astype(BF16)

    id_rows = -(-copies // cols)
    tail = -(-2 * id_rows // 16) * 16
    ids = jnp.stack([dest, key]).astype(BF16)
    ids = jnp.pad(ids, ((0, 0), (0, id_rows * cols - copies))).reshape(2 * id_rows, cols)
    ids = jnp.pad(ids, ((0, tail - 2 * id_rows), (0, 0)))
    own_ids = dest * GO + key

    def half_rows(x, start):
        return lax.dynamic_slice_in_dim(x, start, half, 0)

    starts = (first, other)
    inverse_halves = (kh, ko)
    limit_halves = [half_rows(limit, s)[:, None] for s in starts]
    load_halves = [half_rows(load, s).astype(F32) for s in starts]
    keep_halves = [half_rows(keep, s) for s in starts]

    drive = load
    at = jnp.clip(dot32(kc, load), -limit_c, limit_c)
    dual = jnp.zeros((copies, cols), F32)
    sent = jnp.zeros((copies, cols), F32)
    totals_others = jnp.zeros((copies, cols), F32)
    masks = None
    for iteration in range(ITERS):
        shared = at + dual
        change = (shared - sent).astype(BF16)
        sent = sent + change.astype(F32)
        last = iteration == ITERS - 1
        if iteration == 0:
            arrived = from_others(jnp.concatenate([change, ids], 0), regions)
        else:
            arrived = from_others(change, regions)

        dispatch_halves = [
            jnp.clip(dot32(k, drive), -m, m) for k, m in zip(inverse_halves, limit_halves)
        ]
        if last:
            dispatch = jnp.zeros((buses, cols), F32)
            for s, d in zip(starts, dispatch_halves):
                dispatch = lax.dynamic_update_slice_in_dim(dispatch, d, s, 0)
        else:
            known = jnp.zeros((buses, cols), BF16)
            for s, d, l, k in zip(starts, dispatch_halves, load_halves, keep_halves):
                part = ((l + PROXIMAL * d) * k).astype(BF16)
                known = lax.dynamic_update_slice_in_dim(known, part, s, 0)
            known_c = dot32(kc, known)

        if iteration == 0:
            same = []
            for block in arrived:
                id_block = block[copies:copies + 2 * id_rows].astype(jnp.int32)
                id_block = id_block.reshape(2, id_rows * cols)[:, :copies]
                same.append(own_ids[:, None] == (id_block[0] * GO + id_block[1])[None, :])
            mine = own_ids[:, None] == own_ids[None, :]
            counts = jnp.sum(mine.astype(F32), axis=1, keepdims=True)
            for m in same:
                counts = counts + jnp.sum(m.astype(F32), axis=1, keepdims=True)
            tallies = jnp.maximum(counts, 1.0)
            mine = mine.astype(F32)
            masks = [m.astype(BF16) for m in same]
            arrived = [block[:copies] for block in arrived]
        for m, block in zip(masks, arrived):
            totals_others = totals_others + dot32(m, block)
        totals = dot32(mine, shared, lax.Precision.HIGHEST) + totals_others
        consensus = totals / tallies
        dual = dual + at - consensus
        if not last:
            boundary = consensus - dual
            drive_c = (load_c + PROXIMAL * at + PENALTY * boundary).astype(BF16)
            at = jnp.clip(known_c + dot32(kcc, drive_c), -limit_c, limit_c)
            drive = known + dot32(place, drive_c).astype(BF16)
    return (dispatch[None], dual[None])


def solution(mesh):
    return jax.shard_map(
        per_device,
        mesh=mesh,
        in_specs=(
            P("region", "row", None),
            P("region", None, ("batch", "scen", "row")),
            P("region", None),
            P("region", None),
            P("region", None),
            P("region", None),
            P("region", None),
            P("region", None, None),
        ),
        out_specs=(
            P("region", None, ("batch", "scen", "row")),
            P("region", None, ("batch", "scen", "row")),
        ),
        check_vma=False,
    )
```

time: 116 us -> 44.3 us (0.38); the launches traced: 114 us -> 44 us
  blocking collectives: 43.2 us -> 0 us
  local copies, waits for them, and re-layouts: 17.4 us -> 1.52 us
  matrix products: 3.89 us -> 18.9 us
  other arithmetic: 16.9 us -> 4.17 us
  waiting for transfers between devices: 15.7 us -> 4.99 us
  starting transfers between devices: 16.5 us -> 13.5 us
    all_to_all x5 -> x0, blocking collectives: 35.8 us -> none  [the longest x2 17.8 us: per_device(): lax.all_to_all(packed, 'region', split_axis=0, concat_axis=0, tiled=True)]
    all_to_all x4 -> x0, starting transfers between devices: 16.5 us -> none  [the longest x2 6.65 us: per_device(): lax.all_to_all(replies, 'region', split_axis=0, concat_axis=0, tiled=True)]
    all_to_all x4 -> x0, waiting for transfers between devices: 15.7 us -> none  [the longest x2 7.86 us: per_device(): lax.all_to_all(replies, 'region', split_axis=0, concat_axis=0, tiled=True)]
    dot_general x6 -> x28, matrix products: 3.89 us -> 18.9 us  [dot32(): return jnp.dot(a, b, precision=precision, preferred_element_type=F32)]
    ppermute x0 -> x11, starting transfers between devices: none -> 13.5 us  [the longest x9 12.8 us: from_others(): lax.ppermute(x, 'region', [(i, i ^ s) for i in range(regions)])]
    gather x9 -> x0, local copies, waits for them, and re-layouts: 8.39 us -> none  [the longest x3 3.38 us: per_device(): replies = averages[fetch_rows].reshape(regions, capacity, column_count)]
    scatter-add x3 -> x0, other arithmetic: 7.89 us -> none  [per_device(): boundary = jnp.zeros((bus_count, column_count), jnp.float32).at[local_row...]
    all_gather x3 -> x0, blocking collectives: 7.31 us -> none  [per_device(): lax.all_gather(drive_cols, 'row', axis=1, tiled=True)]
  transfers between devices with their start and end apart: 4 -> 11, of which waited for: 4 -> 4; matrix products, arithmetic and copies ran while one was open for 4% -> 37% of each run, Pallas kernels for 0% -> 0%
where the time goes in v1:
time: 44.3 us; the launch traced here: 44 us
  matrix products  18.9 us (43%)
  starting transfers between devices  13.5 us (30%)
  waiting for transfers between devices  4.99 us (11%)
  other arithmetic  4.17 us (9%)
  local copies, waits for them, and re-layouts  1.52 us (3%)
  between operations  0.97 us (2%)
    dot_general x28, matrix products, dot32(): return jnp.dot(a, b, precision=precision, preferred_element_type=F32)  18.9 us
    ppermute x9, starting transfers between devices, from_others(): lax.ppermute(x, 'region', [(i, i ^ s) for i in range(regions)])  12.8 us
    ppermute x9, waiting for transfers between devices, from_others(): lax.ppermute(x, 'region', [(i, i ^ s) for i in range(regions)])  4.98 us
  transfers between devices with their start and end apart: 11, of which 4 were waited for; matrix products, arithmetic and copies ran while one was open for 37% of the time, Pallas kernels for 0%

profile of v1, /device:TPU:0, one launch (start us, length us, event | category | flops | bytes accessed | tf_op | source)
XLA Modules:
  0.0 44.0 jit_solution(1375386131329063455)
XLA Ops:
  0.7 0.8 %broadcast_subtract_fusion.1 = s32[128]{0:T(128)S(1)} fusion(s32[]{:T(128)S(6)} %mul.76, s32[1,128]{1,0:T(1,128)} %param.11), kind=kLoop, calls=%fused_computation.162 | loop fusion | flops 128 | bytes 1028 | tf_op jit(solution)/shard_map/sub | solution.py:61
  1.5 2.2 %convolution_convert_fusion.2 = bf16[128,1536]{1,0:T(8,128)(2,1)S(1)} fusion(s32[128]{0:T(128)S(1)} %broadcast_subtract_fusion.1, bf16[1,768,1536]{2,1,0:T(8,128)(2,1)} %param.8), kind=kOutput, calls=%fused_computation.2 | convolution fusion | flops 302284800 | bytes 2753024 | tf_op jit(solution)/shard_map/dot_general | solution.py:15
  3.7 0.6 %collective-permute-start.1 = (bf16[128,1536]{1,0:T(8,128)(2,1)S(1)}, bf16[128,1536]{1,0:T(8,128)(2,1)S(1)}, u32[]{:S(2)}, u32[]{:S(2)}) collective-permute-start(bf16[128,1536]{1,0:T(8,128)(2,1)S(1)} %convolution_convert_fusion.2), channel_id=1, source_target_pairs={{0,1},{1,0},{2,3},{3,2},{4,5},{5,4},{6,7},{7,6},{8,9},{9,8},{10,11... | collective-permute-start | bytes 1179656 | tf_op jit(solution)/shard_map/ppermute | solution.py:19
  4.4 0.2 convert_reduce_fusion
  4.6 0.7 %reduce.2 = f32[1536]{0:T(1024)S(1)} reduce(f32[1,1536]{1,0:T(1,128)} %param.10, f32[]{:T(128)} %constant.40), dimensions={0}, to_apply=%param.10.reduce_sub_computation | reduce | bytes 12292 | tf_op args[2]
  5.3 0.9 %select_reduce_fusion = f32[128]{0:T(128)S(1)} fusion(f32[1536]{0:T(1024)S(1)} %reduce.2, s32[128]{0:T(128)} %bitcast.101), kind=kLoop, calls=%fused_computation.69 | loop fusion | flops 589696 | bytes 7168 | tf_op jit(solution)/shard_map/reduce_sum | solution.py:70
  6.2 0.5 %copy-done.3 = f32[128]{0:T(128)} copy-done((f32[128]{0:T(128)}, f32[128]{0:T(128)S(1)}, u32[]{:S(2)}) %copy-start.3) | copy-done | bytes 536
  6.7 0.5 %neg.32 = f32[128]{0:T(128)} negate(f32[128]{0:T(128)S(1)} %select_reduce_fusion) | non-fusion elementwise | flops 128 | bytes 1024 | tf_op jit(solution)/shard_map/neg | solution.py:90
  7.2 1.6 %fusion.51 = f32[128,128]{1,0:T(8,128)} fusion(bf16[1,1536,128]{2,1,0:T(8,128)(2,1)S(1)} %copy-done.2, s32[128]{0:T(128)} %bitcast.102), kind=kOutput, calls=%fused_computation.71 | convolution fusion | flops 50528256 | bytes 459264 | tf_op jit(solution)/shard_map/dot_general | solution.py:15
  8.8 0.7 %dynamic-slice_reduce_fusion = (f32[768]{0:T(1024)S(1)}, f32[768]{0:T(1024)S(1)}) fusion(f32[1,1536]{1,0:T(1,128)} %param.10, s32[]{:T(128)S(6)} %select_n.9, s32[]{:T(128)S(6)} %select_n.8), kind=kLoop, calls=%fused_computation.152 | loop fusion | bytes 12296 | tf_op jit(solution)/shard_map/dynamic_slice | solution.py:81
  9.6 0.7 %add_bitcast_fusion.3 = (s32[128]{0:T(128)S(1)}, bf16[1,128]{1,0:T(2,128)(2,1)S(1)}, bf16[1,128]{1,0:T(2,128)(2,1)S(1)}) fusion(s32[1,128]{1,0:T(1,128)} %param.13, s32[1,128]{1,0:T(1,128)} %param.12), kind=kLoop, calls=%fused_computation.161 | loop fusion | flops 512 | bytes 2048 | tf_op jit(solution)/shard_map/add | solution.py:78
  10.5 0.9 %fusion.33 = bf16[1536,128]{1,0:T(8,128)(2,1)S(1)} fusion(bf16[1536,128]{1,0:T(8,128)(2,1)S(1)} %broadcast.62.clone, s32[]{:T(128)S(6)} %select_n.8, bf16[1,1536,128]{2,1,0:T(8,128)(2,1)S(1)} %copy-done.2, f32[768]{0:T(1024)S(1)} %get-tuple-element.15, f32[768]{0:T(1024)S(1)} %neg.30, f32[768]{0:T(1024)S(1)} %get-tuple-element.3, ...), kind=kOutput, calls=%fused_computation.42 | convolution fusion | flops 302678016 | bytes 3158020 | tf_op jit(solution)/shard_map/dot_general | solution.py:15
  11.5 0.3 fusion.123
  11.7 5.1 %collective-permute-start.4 = (bf16[144,128]{1,0:T(8,128)(2,1)S(1)}, bf16[144,128]{1,0:T(8,128)(2,1)S(1)}, u32[]{:S(2)}, u32[]{:S(2)}) collective-permute-start(bf16[144,128]{1,0:T(8,128)(2,1)S(1)} %pad_maximum_fusion), channel_id=1, source_target_pairs={{0,12},{4,8},{8,4},{12,0},{1,13},{5,9},{9,5},{13,1},{2,14},{6,10},... | collective-permute-start | bytes 110600 | tf_op jit(solution)/shard_map/ppermute | solution.py:25
  16.8 0.6 %collective-permute-start.2 = (bf16[144,128]{1,0:T(8,128)(2,1)S(1)}, bf16[144,128]{1,0:T(8,128)(2,1)S(1)}, u32[]{:S(2)}, u32[]{:S(2)}) collective-permute-start(bf16[144,128]{1,0:T(8,128)(2,1)S(1)} %pad_maximum_fusion), channel_id=1, source_target_pairs={{0,4},{4,0},{8,12},{12,8},{1,5},{5,1},{9,13},{13,9},{2,6},{6,2},{1... | collective-permute-start | bytes 110600 | tf_op jit(solution)/shard_map/ppermute | solution.py:25
  17.5 0.3 convolution_convert_fusion.3
  17.8 1.0 %collective-permute-done.4 = bf16[144,128]{1,0:T(8,128)(2,1)S(1)} collective-permute-done((bf16[144,128]{1,0:T(8,128)(2,1)S(1)}, bf16[144,128]{1,0:T(8,128)(2,1)S(1)}, u32[]{:S(2)}, u32[]{:S(2)}) %collective-permute-start.4) | collective-permute-done | bytes 36896 | tf_op jit(solution)/shard_map/ppermute | solution.py:25
  18.8 2.9 %collective-permute-done.3 = bf16[144,128]{1,0:T(8,128)(2,1)S(1)} collective-permute-done((bf16[144,128]{1,0:T(8,128)(2,1)S(1)}, bf16[144,128]{1,0:T(8,128)(2,1)S(1)}, u32[]{:S(2)}, u32[]{:S(2)}) %collective-permute-start.3) | collective-permute-done | bytes 36896 | tf_op jit(solution)/shard_map/ppermute | solution.py:25
  21.7 0.2 fusion.85
  21.9 0.2 fusion.66
  22.1 0.2 fusion.72
  22.3 0.2 fusion.45
  22.6 0.2 add_convert_fusion.1
  22.9 2.5 %fusion.31 = bf16[1536,128]{1,0:T(8,128)(2,1)S(1)} fusion(bf16[1536,128]{1,0:T(8,128)(2,1)S(1)} %fusion.33, s32[]{:T(128)S(6)} %select_n.9, bf16[768,1536]{1,0:T(8,128)(2,1)} %collective-permute-done, bf16[1,1536,128]{2,1,0:T(8,128)(2,1)S(1)} %copy-done.2, f32[768]{0:T(1024)S(1)} %get-tuple-element.14, f32[768]{0:T(1024)S(1)} %neg.31, ...), kind=kOutput, calls=%fused_computation.40 | convolution fusion | flops 302678016 | bytes 3158020 | tf_op jit(solution)/shard_map/dot_general | solution.py:15
  25.5 0.3 fusion.81
  25.7 2.0 %collective-permute-start.6 = (bf16[128,128]{1,0:T(8,128)(2,1)S(1)}, bf16[128,128]{1,0:T(8,128)(2,1)S(1)}, u32[]{:S(2)}, u32[]{:S(2)}) collective-permute-start(bf16[128,128]{1,0:T(8,128)(2,1)S(1)} %get-tuple-element.10), channel_id=1, source_target_pairs={{0,8},{4,12},{8,0},{12,4},{1,9},{5,13},{9,1},{13,5},{2,10},{6,14},... | collective-permute-start | bytes 98312 | tf_op jit(solution)/shard_map/ppermute | solution.py:25
  27.8 0.5 %collective-permute-start.7 = (bf16[128,128]{1,0:T(8,128)(2,1)S(1)}, bf16[128,128]{1,0:T(8,128)(2,1)S(1)}, u32[]{:S(2)}, u32[]{:S(2)}) collective-permute-start(bf16[128,128]{1,0:T(8,128)(2,1)S(1)} %get-tuple-element.10), channel_id=1, source_target_pairs={{0,12},{4,8},{8,4},{12,0},{1,13},{5,9},{9,5},{13,1},{2,14},{6,10},... | collective-permute-start | bytes 98312 | tf_op jit(solution)/shard_map/ppermute | solution.py:25
  28.3 1.0 %collective-permute-start.5 = (bf16[128,128]{1,0:T(8,128)(2,1)S(1)}, bf16[128,128]{1,0:T(8,128)(2,1)S(1)}, u32[]{:S(2)}, u32[]{:S(2)}) collective-permute-start(bf16[128,128]{1,0:T(8,128)(2,1)S(1)} %get-tuple-element.10), channel_id=1, source_target_pairs={{0,4},{4,0},{8,12},{12,8},{1,5},{5,1},{9,13},{13,9},{2,6},{6,2},{1... | collective-permute-start | bytes 98312 | tf_op jit(solution)/shard_map/ppermute | solution.py:25
  29.3 0.3 fusion
  29.6 0.9 %fusion.29 = bf16[1536,128]{1,0:T(8,128)(2,1)S(1)} fusion(bf16[1536,128]{1,0:T(8,128)(2,1)S(1)} %broadcast.62, s32[]{:T(128)S(6)} %select_n.8, bf16[1536,128]{1,0:T(8,128)(2,1)S(1)} %fusion, f32[768]{0:T(1024)S(1)} %get-tuple-element.15, f32[768]{0:T(1024)S(1)} %neg.30, f32[768]{0:T(1024)S(1)} %get-tuple-element.3, bf16[1,1536,128]{2,1,0:T(8,128)(2,1)S(1)} %copy-done.2, ...), kind=kOutput, calls=%fused_computation.38 | convolution fusion | flops 302678016 | bytes 3158020 | tf_op jit(solution)/shard_map/dot_general | solution.py:15
  30.5 2.5 %fusion.27 = bf16[1536,128]{1,0:T(8,128)(2,1)S(1)} fusion(bf16[1536,128]{1,0:T(8,128)(2,1)S(1)} %fusion.29, s32[]{:T(128)S(6)} %select_n.9, bf16[768,1536]{1,0:T(8,128)(2,1)} %collective-permute-done, bf16[1536,128]{1,0:T(8,128)(2,1)S(1)} %fusion, f32[768]{0:T(1024)S(1)} %neg.31, f32[768]{0:T(1024)S(1)} %get-tuple-element.2, ...), kind=kOutput, calls=%fused_computation.36 | convolution fusion | flops 302678016 | bytes 3158020 | tf_op jit(solution)/shard_map/dot_general | solution.py:15
  33.0 0.2 fusion.70
  33.2 0.3 collective-permute-done.7
  33.5 0.2 fusion.64
  33.7 0.2 fusion.41
  33.9 0.2 add_convert_fusion
  34.3 0.3 fusion.83
  34.6 2.7 %collective-permute-start.9 = (bf16[128,128]{1,0:T(8,128)(2,1)S(1)}, bf16[128,128]{1,0:T(8,128)(2,1)S(1)}, u32[]{:S(2)}, u32[]{:S(2)}) collective-permute-start(bf16[128,128]{1,0:T(8,128)(2,1)S(1)} %get-tuple-element.22), channel_id=1, source_target_pairs={{0,8},{4,12},{8,0},{12,4},{1,9},{5,13},{9,1},{13,5},{2,10},{6,14},... | collective-permute-start | bytes 98312 | tf_op jit(solution)/shard_map/ppermute | solution.py:25
  37.2 0.5 %collective-permute-start.10 = (bf16[128,128]{1,0:T(8,128)(2,1)S(1)}, bf16[128,128]{1,0:T(8,128)(2,1)S(1)}, u32[]{:S(2)}, u32[]{:S(2)}) collective-permute-start(bf16[128,128]{1,0:T(8,128)(2,1)S(1)} %get-tuple-element.22), channel_id=1, source_target_pairs={{0,12},{4,8},{8,4},{12,0},{1,13},{5,9},{9,5},{13,1},{2,14},{6,10},... | collective-permute-start | bytes 98312 | tf_op jit(solution)/shard_map/ppermute | solution.py:25
  37.8 0.4 collective-permute-start.8
  38.1 0.3 fusion.1
  38.4 0.8 %fusion.22 = f32[1,1536,128]{2,1,0:T(8,128)S(1)} fusion(f32[1,1536,128]{2,1,0:T(8,128)S(1)} %broadcast_in_dim.22, s32[]{:T(128)S(6)} %select_n.8, bf16[1536,128]{1,0:T(8,128)(2,1)S(1)} %fusion.1, f32[768]{0:T(1024)S(1)} %neg.30, f32[768]{0:T(1024)S(1)} %get-tuple-element.3, bf16[1,768,1536]{2,1,0:T(8,128)(2,1)S(1)} %copy-done), kind=kOutput, calls=%fused_computation.31 | convolution fusion | flops 302186496 | bytes 3153924 | tf_op jit(solution)/shard_map/dot_general | solution.py:15
  39.2 2.4 %fusion.25 = f32[1,1536,128]{2,1,0:T(8,128)S(1)} fusion(f32[1,1536,128]{2,1,0:T(8,128)S(1)} %fusion.22, s32[]{:T(128)S(6)} %select_n.9, bf16[768,1536]{1,0:T(8,128)(2,1)} %collective-permute-done, bf16[1536,128]{1,0:T(8,128)(2,1)S(1)} %fusion.1, f32[768]{0:T(1024)S(1)} %neg.31, f32[768]{0:T(1024)S(1)} %get-tuple-element.2), kind=kOutput, calls=%fused_computation.34 | convolution fusion | flops 302186496 | bytes 3153924 | tf_op jit(solution)/shard_map/dot_general | solution.py:15
  41.7 0.2 fusion.77
  41.9 0.2 fusion.68
  42.1 0.8 %collective-permute-done.10 = bf16[128,128]{1,0:T(8,128)(2,1)S(1)} collective-permute-done((bf16[128,128]{1,0:T(8,128)(2,1)S(1)}, bf16[128,128]{1,0:T(8,128)(2,1)S(1)}, u32[]{:S(2)}, u32[]{:S(2)}) %collective-permute-start.10) | collective-permute-done | bytes 32800 | tf_op jit(solution)/shard_map/ppermute | solution.py:25
  42.9 0.2 fusion.62
  43.1 0.8 %fusion.50 = f32[1,128,128]{2,1,0:T(8,128)} fusion(f32[128,128]{1,0:T(8,128)S(1)} %get-tuple-element.23, f32[128,128]{1,0:T(8,128)S(1)} %fusion.77, f32[128,128]{1,0:T(8,128)S(1)} %fusion.62, f32[128,128]{1,0:T(8,128)S(1)} %fusion.68, f32[128,128]{1,0:T(8,128)S(1)} %fusion.41, bf16[128,128]{1,0:T(8,128)(2,1)S(1)} %collective-permute-done.8, ...), kind=kOutput, calls=%fused_computation.67 | convolution fusion | flops 4308992 | bytes 427520 | tf_op jit(solution)/shard_map/dot_general | solution.py:15
  (45 shorter events, 0.8 us)
Async XLA Ops:
  0.6 3.8 %copy-start.5 = (s32[1,128]{1,0:T(1,128)S(1)}, s32[1,128]{1,0:T(1,128)}, u32[]{:S(2)}) copy-start(s32[1,128]{1,0:T(1,128)} %param.11) | copy-start | bytes 1540
  0.6 3.7 %copy-start = (bf16[1,768,1536]{2,1,0:T(8,128)(2,1)S(1)}, bf16[1,768,1536]{2,1,0:T(8,128)(2,1)}, u32[]{:S(2)}) copy-start(bf16[1,768,1536]{2,1,0:T(8,128)(2,1)} %param.8) | copy-start | bytes 7077892
  0.7 6.5 %copy-start.2 = (bf16[1,1536,128]{2,1,0:T(8,128)(2,1)S(1)}, bf16[1,1536,128]{2,1,0:T(8,128)(2,1)}, u32[]{:S(2)}) copy-start(bf16[1,1536,128]{2,1,0:T(8,128)(2,1)} %param.9) | copy-start | bytes 1179652
  3.7 7.6 %collective-permute-start.1 = (bf16[128,1536]{1,0:T(8,128)(2,1)S(1)}, bf16[128,1536]{1,0:T(8,128)(2,1)S(1)}, u32[]{:S(2)}, u32[]{:S(2)}) collective-permute-start(bf16[128,1536]{1,0:T(8,128)(2,1)S(1)} %convolution_convert_fusion.2), channel_id=1, source_target_pairs={{0,1},{1,0},{2,3},{3,2},{4,5},{5,4},{6,7},{7,6},{8,9},{9,8},{10,11... | collective-permute-start | bytes 1179656 | tf_op jit(solution)/shard_map/ppermute | solution.py:19
  4.3 18.6 %collective-permute-start = (bf16[768,1536]{1,0:T(8,128)(2,1)S(1)}, bf16[768,1536]{1,0:T(8,128)(2,1)}, u32[]{:S(2)}, u32[]{:S(2)}) collective-permute-start(bf16[768,1536]{1,0:T(8,128)(2,1)S(1)} %bitcast.100), channel_id=1, source_target_pairs={{0,1},{1,0},{2,3},{3,2},{4,5},{5,4},{6,7},{7,6},{8,9},{9,8},{10,11... | collective-permute-start | bytes 7077896 | tf_op jit(solution)/shard_map/ppermute | solution.py:19
  6.2 0.5 %copy-start.3 = (f32[128]{0:T(128)}, f32[128]{0:T(128)S(1)}, u32[]{:S(2)}) copy-start(f32[128]{0:T(128)S(1)} %select_reduce_fusion) | copy-start | bytes 1540
  10.4 1.0 %copy-start.4 = (f32[128]{0:T(128)S(1)}, f32[128]{0:T(128)}, u32[]{:S(2)}) copy-start(f32[128]{0:T(128)} %copy-done.3) | copy-start | bytes 1540
  10.4 1.0 %copy-start.7 = (f32[128]{0:T(128)S(1)}, f32[128]{0:T(128)}, u32[]{:S(2)}) copy-start(f32[128]{0:T(128)} %neg.32) | copy-start | bytes 1540
  10.5 7.0 %copy-start.6 = (s32[1,128]{1,0:T(1,128)S(1)}, s32[1,128]{1,0:T(1,128)}, u32[]{:S(2)}) copy-start(s32[1,128]{1,0:T(1,128)} %param.11) | copy-start | bytes 1540
  11.3 11.2 %copy-start.8 = (f32[128,128]{1,0:T(8,128)S(1)}, f32[128,128]{1,0:T(8,128)}, u32[]{:S(2)}) copy-start(f32[128,128]{1,0:T(8,128)} %fusion.51) | copy-start | bytes 196612
  11.7 7.0 %collective-permute-start.4 = (bf16[144,128]{1,0:T(8,128)(2,1)S(1)}, bf16[144,128]{1,0:T(8,128)(2,1)S(1)}, u32[]{:S(2)}, u32[]{:S(2)}) collective-permute-start(bf16[144,128]{1,0:T(8,128)(2,1)S(1)} %pad_maximum_fusion), channel_id=1, source_target_pairs={{0,12},{4,8},{8,4},{12,0},{1,13},{5,9},{9,5},{13,1},{2,14},{6,10},... | collective-permute-start | bytes 110600 | tf_op jit(solution)/shard_map/ppermute | solution.py:25
  16.8 4.9 %collective-permute-start.3 = (bf16[144,128]{1,0:T(8,128)(2,1)S(1)}, bf16[144,128]{1,0:T(8,128)(2,1)S(1)}, u32[]{:S(2)}, u32[]{:S(2)}) collective-permute-start(bf16[144,128]{1,0:T(8,128)(2,1)S(1)} %pad_maximum_fusion), channel_id=1, source_target_pairs={{0,8},{4,12},{8,0},{12,4},{1,9},{5,13},{9,1},{13,5},{2,10},{6,14},... | collective-permute-start | bytes 110600 | tf_op jit(solution)/shard_map/ppermute | solution.py:25
  16.8 4.9 %collective-permute-start.2 = (bf16[144,128]{1,0:T(8,128)(2,1)S(1)}, bf16[144,128]{1,0:T(8,128)(2,1)S(1)}, u32[]{:S(2)}, u32[]{:S(2)}) collective-permute-start(bf16[144,128]{1,0:T(8,128)(2,1)S(1)} %pad_maximum_fusion), channel_id=1, source_target_pairs={{0,4},{4,0},{8,12},{12,8},{1,5},{5,1},{9,13},{13,9},{2,6},{6,2},{1... | collective-permute-start | bytes 110600 | tf_op jit(solution)/shard_map/ppermute | solution.py:25
  25.7 7.3 %collective-permute-start.6 = (bf16[128,128]{1,0:T(8,128)(2,1)S(1)}, bf16[128,128]{1,0:T(8,128)(2,1)S(1)}, u32[]{:S(2)}, u32[]{:S(2)}) collective-permute-start(bf16[128,128]{1,0:T(8,128)(2,1)S(1)} %get-tuple-element.10), channel_id=1, source_target_pairs={{0,8},{4,12},{8,0},{12,4},{1,9},{5,13},{9,1},{13,5},{2,10},{6,14},... | collective-permute-start | bytes 98312 | tf_op jit(solution)/shard_map/ppermute | solution.py:25
  27.8 5.7 %collective-permute-start.7 = (bf16[128,128]{1,0:T(8,128)(2,1)S(1)}, bf16[128,128]{1,0:T(8,128)(2,1)S(1)}, u32[]{:S(2)}, u32[]{:S(2)}) collective-permute-start(bf16[128,128]{1,0:T(8,128)(2,1)S(1)} %get-tuple-element.10), channel_id=1, source_target_pairs={{0,12},{4,8},{8,4},{12,0},{1,13},{5,9},{9,5},{13,1},{2,14},{6,10},... | collective-permute-start | bytes 98312 | tf_op jit(solution)/shard_map/ppermute | solution.py:25
  28.3 5.4 %collective-permute-start.5 = (bf16[128,128]{1,0:T(8,128)(2,1)S(1)}, bf16[128,128]{1,0:T(8,128)(2,1)S(1)}, u32[]{:S(2)}, u32[]{:S(2)}) collective-permute-start(bf16[128,128]{1,0:T(8,128)(2,1)S(1)} %get-tuple-element.10), channel_id=1, source_target_pairs={{0,4},{4,0},{8,12},{12,8},{1,5},{5,1},{9,13},{13,9},{2,6},{6,2},{1... | collective-permute-start | bytes 98312 | tf_op jit(solution)/shard_map/ppermute | solution.py:25
  34.6 7.4 %collective-permute-start.9 = (bf16[128,128]{1,0:T(8,128)(2,1)S(1)}, bf16[128,128]{1,0:T(8,128)(2,1)S(1)}, u32[]{:S(2)}, u32[]{:S(2)}) collective-permute-start(bf16[128,128]{1,0:T(8,128)(2,1)S(1)} %get-tuple-element.22), channel_id=1, source_target_pairs={{0,8},{4,12},{8,0},{12,4},{1,9},{5,13},{9,1},{13,5},{2,10},{6,14},... | collective-permute-start | bytes 98312 | tf_op jit(solution)/shard_map/ppermute | solution.py:25
  37.2 5.7 %collective-permute-start.10 = (bf16[128,128]{1,0:T(8,128)(2,1)S(1)}, bf16[128,128]{1,0:T(8,128)(2,1)S(1)}, u32[]{:S(2)}, u32[]{:S(2)}) collective-permute-start(bf16[128,128]{1,0:T(8,128)(2,1)S(1)} %get-tuple-element.22), channel_id=1, source_target_pairs={{0,12},{4,8},{8,4},{12,0},{1,13},{5,9},{9,5},{13,1},{2,14},{6,10},... | collective-permute-start | bytes 98312 | tf_op jit(solution)/shard_map/ppermute | solution.py:25
  37.8 5.4 %collective-permute-start.8 = (bf16[128,128]{1,0:T(8,128)(2,1)S(1)}, bf16[128,128]{1,0:T(8,128)(2,1)S(1)}, u32[]{:S(2)}, u32[]{:S(2)}) collective-permute-start(bf16[128,128]{1,0:T(8,128)(2,1)S(1)} %get-tuple-element.22), channel_id=1, source_target_pairs={{0,4},{4,0},{8,12},{12,8},{1,5},{5,1},{9,13},{13,9},{2,6},{6,2},{1... | collective-permute-start | bytes 98312 | tf_op jit(solution)/shard_map/ppermute | solution.py:25
  41.7 2.3 %copy-start.1 = (f32[1,1536,128]{2,1,0:T(8,128)}, f32[1,1536,128]{2,1,0:T(8,128)S(1)}, u32[]{:S(2)}) copy-start(f32[1,1536,128]{2,1,0:T(8,128)S(1)} %fusion.25) | copy-start | bytes 2359300

commit v2 on v0

v2 whole, which is shorter than its diff:
```python
import functools

import jax
import jax.numpy as jnp
from jax import lax
from jax.experimental import pallas as pl
from jax.experimental.pallas import tpu as pltpu
from jax.sharding import PartitionSpec as P

GO = 64
ITERS = 3
PENALTY = 1.0
PROXIMAL = 0.5
TAIL = 16
F32 = jnp.float32
BF16 = jnp.bfloat16
VMEM = pl.BlockSpec(memory_space=pltpu.VMEM)


def dot32(a, b, precision=None):
    return jnp.dot(a, b, precision=precision, preferred_element_type=F32)


def in_vmem(body, outs, *operands):
    return pl.pallas_call(
        body,
        out_shape=[pltpu.VMEM(shape, dtype) for shape, dtype in outs],
        in_specs=[VMEM] * len(operands),
        out_specs=[VMEM] * len(outs),
        compiler_params=pltpu.CompilerParams(vmem_limit_bytes=12 << 20),
    )(*[pltpu.with_memory_space_constraint(x, pltpu.VMEM) for x in operands])


def column(row):
    size = row.shape[1]
    return jnp.broadcast_to(row.astype(F32), (size, size)).T


def lanes(shape, offset=0):
    return (lax.broadcasted_iota(jnp.int32, shape, 1) + offset).astype(F32)


def ones_where(condition):
    return jnp.where(condition, 1.0, 0.0).astype(BF16)


def halves(half):
    first = lax.axis_index("row") * half
    return (
        pl.ds(pl.multiple_of(first, half), half),
        pl.ds(pl.multiple_of(half - first, half), half),
    )


def gather_kernel(local_ref, own_ref, part_ref):
    half = own_ref.shape[0]
    wanted = column(local_ref[...]) - (lax.axis_index("row") * half).astype(F32)
    copies = wanted.shape[0]
    pick = jnp.concatenate(
        [ones_where(wanted == lanes(wanted.shape, c)) for c in range(0, half, copies)], 1
    )
    part_ref[...] = dot32(pick, own_ref[...]).astype(BF16)


def tables_kernel(
    local_ref, limit_ref, load_ref, place_ref, bound_ref, keep_ref, load_c_ref, bound_c_ref
):
    buses, cols = load_ref.shape
    local = local_ref[...]
    copies = local.shape[1]
    place = ones_where(lax.broadcasted_iota(jnp.int32, (buses, copies), 0) == local)
    place_ref[...] = place
    keep_ref[...] = 1.0 - dot32(place, jnp.ones((copies, cols), BF16))
    wanted = column(local)
    picks = []
    limits = jnp.zeros((copies, copies), F32)
    for c in range(0, buses, copies):
        limit = limit_ref[:, c:c + copies]
        bound_ref[c:c + copies, :] = jnp.broadcast_to(limit, (cols, copies)).T
        hit = wanted == lanes(wanted.shape, c)
        picks.append(ones_where(hit))
        limits = limits + jnp.where(hit, limit, 0.0)
    load_c_ref[...] = dot32(jnp.concatenate(picks, 1), load_ref[...])
    bound_c_ref[...] = jnp.broadcast_to(jnp.sum(limits, 1, keepdims=True), (copies, cols))


def first_kernel(
    part_ref, other_ref, load_ref, bound_c_ref, dest_ref, key_ref, rows_ref, at_ref, sent_ref,
    message_ref,
):
    rows = (part_ref[...].astype(F32) + other_ref[...].astype(F32)).astype(BF16)
    rows_ref[...] = rows
    bound = bound_c_ref[...]
    at = jnp.clip(dot32(rows, load_ref[...]), -bound, bound)
    at_ref[...] = at
    copies, cols = at.shape
    message = at.astype(BF16)
    sent_ref[...] = message.astype(F32)
    message_ref[:copies, :] = message
    line = lax.broadcasted_iota(jnp.int32, (TAIL, cols), 0)
    ids = jnp.where(line == 0, dest_ref[...], jnp.where(line == 1, key_ref[...], 0))
    message_ref[copies:, :] = ids.astype(F32).astype(BF16)


def own_ids(dest_ref, key_ref):
    return (dest_ref[...] * GO + key_ref[...]).astype(F32)


def own_total(dest_ref, key_ref, shared_ref):
    ids = own_ids(dest_ref, key_ref)
    mine = jnp.where(column(ids) == ids, 1.0, 0.0)
    return dot32(mine, shared_ref[...], lax.Precision.HIGHEST)


def solve_all(own_ref, swapped_ref, drive, bound_ref):
    half = own_ref.shape[0]
    for rows, part_ref in zip(halves(half), (own_ref, swapped_ref)):
        bound = bound_ref[rows, :]
        yield rows, jnp.clip(dot32(part_ref[...], drive), -bound, bound)


def known_part(
    own_ref, swapped_ref, drive, bound_ref, keep_ref, load_ref, rows_ref, known_ref, known_c_ref
):
    for rows, dispatch in solve_all(own_ref, swapped_ref, drive, bound_ref):
        known = (load_ref[rows, :].astype(F32) + PROXIMAL * dispatch) * keep_ref[rows, :]
        known_ref[rows, :] = known.astype(BF16)
    known_c_ref[...] = dot32(rows_ref[...], known_ref[...])


def first_solve_kernel(
    own_ref, swapped_ref, load_ref, bound_ref, keep_ref, rows_ref, place_ref, dest_ref, key_ref,
    shared_ref, known_ref, known_c_ref, block_ref, own_total_ref,
):
    own_total_ref[...] = own_total(dest_ref, key_ref, shared_ref)
    block_ref[...] = dot32(rows_ref[...], place_ref[...]).astype(BF16)
    known_part(
        own_ref, swapped_ref, load_ref[...], bound_ref, keep_ref, load_ref, rows_ref, known_ref,
        known_c_ref,
    )


def drive_of(known_ref, place_ref, drive_c_ref):
    return known_ref[...] + dot32(place_ref[...], drive_c_ref[...]).astype(BF16)


def next_solve_kernel(
    own_ref, swapped_ref, load_ref, bound_ref, keep_ref, rows_ref, place_ref, dest_ref, key_ref,
    shared_ref, before_ref, drive_c_ref, known_ref, known_c_ref, own_total_ref,
):
    own_total_ref[...] = own_total(dest_ref, key_ref, shared_ref)
    drive = drive_of(before_ref, place_ref, drive_c_ref)
    known_part(
        own_ref, swapped_ref, drive, bound_ref, keep_ref, load_ref, rows_ref, known_ref,
        known_c_ref,
    )


def last_solve_kernel(
    own_ref, swapped_ref, bound_ref, place_ref, dest_ref, key_ref, shared_ref, before_ref,
    drive_c_ref, dispatch_ref, own_total_ref,
):
    own_total_ref[...] = own_total(dest_ref, key_ref, shared_ref)
    drive = drive_of(before_ref, place_ref, drive_c_ref)
    for rows, dispatch in solve_all(own_ref, swapped_ref, drive, bound_ref):
        dispatch_ref[rows, :] = dispatch


def advance(
    consensus, dual, at_ref, load_c_ref, bound_c_ref, known_c_ref, block_ref, sent_ref, change_ref,
    drive_c_ref, at_out_ref, dual_out_ref, shared_ref, sent_out_ref,
):
    at = at_ref[...]
    dual = dual + at - consensus
    boundary = consensus - dual
    drive_c = (load_c_ref[...] + PROXIMAL * at + PENALTY * boundary).astype(BF16)
    bound = bound_c_ref[...]
    at = jnp.clip(known_c_ref[...] + dot32(block_ref[...], drive_c), -bound, bound)
    shared = at + dual
    sent = sent_ref[...]
    change = (shared - sent).astype(BF16)
    change_ref[...] = change
    sent_out_ref[...] = sent + change.astype(F32)
    drive_c_ref[...] = drive_c
    at_out_ref[...] = at
    dual_out_ref[...] = dual
    shared_ref[...] = shared


def first_mean_kernel(others, *refs):
    blocks, refs = refs[:others], refs[others:]
    (dest_ref, key_ref, own_total_ref, at_ref, load_c_ref, bound_c_ref, known_c_ref, block_ref,
     sent_ref), refs = refs[:9], refs[9:]
    masks_ref, tally_ref, totals_ref = refs[:3]
    ids = own_ids(dest_ref, key_ref)
    copies = ids.shape[1]
    wanted = column(ids)
    count = jnp.where(wanted == ids, 1.0, 0.0)
    masks = []
    for block in blocks:
        theirs = block[copies:copies + 2, :].astype(F32)
        mask = jnp.where(wanted == theirs[0:1] * GO + theirs[1:2], 1.0, 0.0)
        count = count + mask
        masks.append(mask.astype(BF16))
    mask = jnp.concatenate(masks, 1)
    masks_ref[...] = mask
    tally = jnp.broadcast_to(
        jnp.maximum(jnp.sum(count, 1, keepdims=True), 1.0), tally_ref.shape
    )
    tally_ref[...] = tally
    totals = dot32(mask, jnp.concatenate([block[:copies, :] for block in blocks], 0))
    totals_ref[...] = totals
    consensus = (own_total_ref[...] + totals) / tally
    advance(
        consensus, 0.0, at_ref, load_c_ref, bound_c_ref, known_c_ref, block_ref, sent_ref,
        *refs[3:],
    )


def others_total(blocks, masks_ref, totals_ref):
    arrived = jnp.concatenate([block[...] for block in blocks], 0)
    return totals_ref[...] + dot32(masks_ref[...], arrived)


def next_mean_kernel(others, *refs):
    blocks, refs = refs[:others], refs[others:]
    (masks_ref, tally_ref, totals_ref, dual_ref, own_total_ref, at_ref, load_c_ref, bound_c_ref,
     known_c_ref, block_ref, sent_ref), refs = refs[:11], refs[11:]
    totals = others_total(blocks, masks_ref, totals_ref)
    refs[0][...] = totals
    consensus = (own_total_ref[...] + totals) / tally_ref[...]
    advance(
        consensus, dual_ref[...], at_ref, load_c_ref, bound_c_ref, known_c_ref, block_ref,
        sent_ref, *refs[1:],
    )


def last_mean_kernel(others, *refs):
    blocks, refs = refs[:others], refs[others:]
    masks_ref, tally_ref, totals_ref, dual_ref, own_total_ref, at_ref, out_ref = refs
    totals = others_total(blocks, masks_ref, totals_ref)
    consensus = (own_total_ref[...] + totals) / tally_ref[...]
    out_ref[...] = dual_ref[...] + at_ref[...] - consensus


def swap_row(x):
    return lax.ppermute(x, "row", [(0, 1), (1, 0)])


def from_others(x, regions):
    if regions & (regions - 1) == 0 and regions <= 8:
        return [
            lax.ppermute(x, "region", [(i, i ^ s) for i in range(regions)])
            for s in range(1, regions)
        ]
    everyone = lax.all_gather(x, "region", axis=0)
    me = lax.axis_index("region")
    return [
        lax.dynamic_index_in_dim(everyone, lax.rem(me + s, regions), 0, keepdims=False)
        for s in range(1, regions)
    ]


def per_device(
    kkt_inverse, bus_load, bus_limit, copy_local, copy_dest, copy_slot, copy_key, own_key
):
    del copy_slot, own_key
    own = kkt_inverse[0]
    load = bus_load[0]
    regions = lax.axis_size("region")
    others = regions - 1
    half, buses = own.shape
    cols = load.shape[1]
    copies = copy_local.shape[1]
    small = ((copies, cols), F32)
    small16 = ((copies, cols), BF16)

    (part,) = in_vmem(gather_kernel, [((copies, buses), BF16)], copy_local, own)
    other = swap_row(part)
    swapped = swap_row(own)
    place, bound, keep, load_c, bound_c = in_vmem(
        tables_kernel,
        [((buses, copies), BF16), ((buses, cols), F32), ((buses, cols), F32), small, small],
        copy_local, bus_limit, load,
    )
    rows, at, sent, message = in_vmem(
        first_kernel,
        [((copies, buses), BF16), small, small, ((copies + TAIL, cols), BF16)],
        part, other, load, bound_c, copy_dest, copy_key,
    )
    arrived = from_others(message, regions)
    known, known_c, block, own_sum = in_vmem(
        first_solve_kernel,
        [((buses, cols), BF16), small, ((copies, copies), BF16), small],
        own, swapped, load, bound, keep, rows, place, copy_dest, copy_key, at,
    )
    masks, tally, totals, change, drive_c, at, dual, shared, sent = in_vmem(
        functools.partial(first_mean_kernel, others),
        [((copies, others * copies), BF16), small, small, small16, small16] + [small] * 4,
        *arrived, copy_dest, copy_key, own_sum, at, load_c, bound_c, known_c, block, sent,
    )
    for iteration in range(1, ITERS):
        arrived = from_others(change, regions)
        if iteration < ITERS - 1:
            known, known_c, own_sum = in_vmem(
                next_solve_kernel,
                [((buses, cols), BF16), small, small],
                own, swapped, load, bound, keep, rows, place, copy_dest, copy_key, shared, known,
                drive_c,
            )
            totals, change, drive_c, at, dual, shared, sent = in_vmem(
                functools.partial(next_mean_kernel, others),
                [small, small16, small16] + [small] * 4,
                *arrived, masks, tally, totals, dual, own_sum, at, load_c, bound_c, known_c,
                block, sent,
            )
        else:
            dispatch, own_sum = in_vmem(
                last_solve_kernel,
                [((buses, cols), F32), small],
                own, swapped, bound, place, copy_dest, copy_key, shared, known, drive_c,
            )
            (dual,) = in_vmem(
                functools.partial(last_mean_kernel, others),
                [small],
                *arrived, masks, tally, totals, dual, own_sum, at,
            )
    return (dispatch[None], dual[None])


def solution(mesh):
    return jax.shard_map(
        per_device,
        mesh=mesh,
        in_specs=(
            P("region", "row", None),
            P("region", None, ("batch", "scen", "row")),
            P("region", None),
            P("region", None),
            P("region", None),
            P("region", None),
            P("region", None),
            P("region", None, None),
        ),
        out_specs=(
            P("region", None, ("batch", "scen", "row")),
            P("region", None, ("batch", "scen", "row")),
        ),
        check_vma=False,
    )
```

time: 116 us -> 32.8 us (0.28); the launches traced: 114 us -> 32.6 us
  blocking collectives: 43.2 us -> 0 us
  other arithmetic: 16.9 us -> 0 us
  local copies, waits for them, and re-layouts: 17.4 us -> 4.92 us
  waiting for transfers between devices: 15.7 us -> 3.58 us
  Pallas kernels: 0 us -> 8.18 us
  matrix products: 3.89 us -> 0 us
  starting transfers between devices: 16.5 us -> 15.1 us
    all_to_all x5 -> x0, blocking collectives: 35.8 us -> none  [the longest x2 17.8 us: per_device(): lax.all_to_all(packed, 'region', split_axis=0, concat_axis=0, tiled=True)]
    all_to_all x4 -> x0, starting transfers between devices: 16.5 us -> none  [the longest x2 6.65 us: per_device(): lax.all_to_all(replies, 'region', split_axis=0, concat_axis=0, tiled=True)]
    all_to_all x4 -> x0, waiting for transfers between devices: 15.7 us -> none  [the longest x2 7.86 us: per_device(): lax.all_to_all(replies, 'region', split_axis=0, concat_axis=0, tiled=True)]
    ppermute x0 -> x11, starting transfers between devices: none -> 15.1 us  [the longest x9 14.5 us: from_others(): lax.ppermute(x, 'region', [(i, i ^ s) for i in range(regions)])]
    gather x9 -> x0, local copies, waits for them, and re-layouts: 8.39 us -> none  [the longest x3 3.38 us: per_device(): replies = averages[fetch_rows].reshape(regions, capacity, column_count)]
    pallas_call x0 -> x9, Pallas kernels: none -> 8.18 us  [in_vmem(): pl.pallas_call(body, out_shape=[pltpu.VMEM(shape, dtype) for shape, dtype...]
    scatter-add x3 -> x0, other arithmetic: 7.89 us -> none  [per_device(): boundary = jnp.zeros((bus_count, column_count), jnp.float32).at[local_row...]
    all_gather x3 -> x0, blocking collectives: 7.31 us -> none  [per_device(): lax.all_gather(drive_cols, 'row', axis=1, tiled=True)]
  transfers between devices with their start and end apart: 4 -> 11, of which waited for: 4 -> 6; matrix products, arithmetic and copies ran while one was open for 4% -> 3% of each run, Pallas kernels for 0% -> 20%
where the time goes in v2:
time: 32.8 us; the launch traced here: 32.6 us
  starting transfers between devices  15.1 us (46%)
  Pallas kernels  8.18 us (25%)
  local copies, waits for them, and re-layouts  4.92 us (15%)
  waiting for transfers between devices  3.58 us (11%)
  between operations  0.73 us (2%)
    ppermute x9, starting transfers between devices, from_others(): lax.ppermute(x, 'region', [(i, i ^ s) for i in range(regions)])  14.5 us
    pallas_call x9, Pallas kernels, in_vmem(): pl.pallas_call(body, out_shape=[pltpu.VMEM(shape, dtype) for shape, dtype...  8.18 us
    unnamed x16, local copies, waits for them, and re-layouts  4.92 us
    ppermute x9, waiting for transfers between devices, from_others(): lax.ppermute(x, 'region', [(i, i ^ s) for i in range(regions)])  3.07 us
  transfers between devices with their start and end apart: 11, of which 6 were waited for; matrix products, arithmetic and copies ran while one was open for 3% of the time, Pallas kernels for 20%

profile of v2, /device:TPU:0, one launch (start us, length us, event | category | flops | bytes accessed | tf_op | source)
XLA Modules:
  0.0 32.6 jit_solution(7664828986430587394)
XLA Ops:
  0.6 0.0 copy-start.4
  0.6 0.0 copy-start.3
  0.7 0.6 %collective-permute-start = (bf16[768,1536]{1,0:T(8,128)(2,1)}, bf16[768,1536]{1,0:T(8,128)(2,1)S(1)}, u32[]{:S(2)}, u32[]{:S(2)}) collective-permute-start(bf16[768,1536]{1,0:T(8,128)(2,1)} %bitcast.6), channel_id=1, source_target_pairs={{0,1},{1,0},{2,3},{3,2},{4,5},{5,4},{6,7},{7,6},{8,9},{9,8},{10,11... | collective-permute-start | bytes 7077896 | tf_op jit(solution)/shard_map/ppermute | solution.py:247
  1.2 0.0 copy-start
  1.2 1.7 %copy-done = bf16[1,768,1536]{2,1,0:T(8,128)(2,1)S(1)} copy-done((bf16[1,768,1536]{2,1,0:T(8,128)(2,1)S(1)}, bf16[1,768,1536]{2,1,0:T(8,128)(2,1)}, u32[]{:S(2)}) %copy-start) | copy-done | bytes 2359320
  2.9 0.0 copy-start.6
  2.9 0.7 %copy-done.6 = s32[1,128]{1,0:T(1,128)S(1)} copy-done((s32[1,128]{1,0:T(1,128)S(1)}, s32[1,128]{1,0:T(1,128)}, u32[]{:S(2)}) %copy-start.6) | copy-done | bytes 536
  3.5 0.0 copy-start.2
  3.5 0.0 copy-start.1
  3.5 0.5 %shard_map.78.part_ref = bf16[128,1536]{1,0:T(8,128)(2,1)S(1)} custom-call(s32[1,128]{1,0:T(1,128)S(1)} %copy-done.6, bf16[768,1536]{1,0:T(8,128)(2,1)S(1)} %bitcast.7), custom_call_target="tpu_custom_call" | custom-call | tf_op jit(solution)/shard_map/pallas_call | solution.py:25
  4.1 0.1 collective-permute-start.1
  4.1 0.4 %copy-done.2 = bf16[1,1536,128]{2,1,0:T(8,128)(2,1)S(1)} copy-done((bf16[1,1536,128]{2,1,0:T(8,128)(2,1)S(1)}, bf16[1,1536,128]{2,1,0:T(8,128)(2,1)}, u32[]{:S(2)}) %copy-start.2) | copy-done | bytes 393240
  4.5 0.0 copy-start.5
  4.5 0.7 %copy-done.5 = f32[1,1536]{1,0:T(1,128)S(1)} copy-done((f32[1,1536]{1,0:T(1,128)S(1)}, f32[1,1536]{1,0:T(1,128)}, u32[]{:S(2)}) %copy-start.5) | copy-done | bytes 6168
  5.2 0.4 %shard_map.77 = (bf16[1536,128]{1,0:T(8,128)(2,1)S(1)}, f32[1536,128]{1,0:T(8,128)S(1)}, f32[1536,128]{1,0:T(8,128)S(1)}, f32[128,128]{1,0:T(8,128)S(1)}, f32[128,128]{1,0:T(8,128)S(1)}) custom-call(s32[1,128]{1,0:T(1,128)S(1)} %copy-done.6, f32[1,1536]{1,0:T(1,128)S(1)} %copy-done.5, bf16[1536,128]{1,0:T(8,128)(2,1)S(1)} %bitcast.11), custom_call_target="tpu_custom_call" | custom-call | tf_op jit(solution)/shard_map/pallas_call | solution.py:25
  5.6 0.5 %collective-permute-done.1.other_ref = bf16[128,1536]{1,0:T(8,128)(2,1)S(1)} collective-permute-done((bf16[128,1536]{1,0:T(8,128)(2,1)S(1)}, bf16[128,1536]{1,0:T(8,128)(2,1)S(1)}, u32[]{:S(2)}, u32[]{:S(2)}) %collective-permute-start.1) | collective-permute-done | bytes 393248 | tf_op jit(solution)/shard_map/ppermute | solution.py:247
  6.1 0.0 copy-done.4
  6.1 0.0 copy-done.3
  6.1 0.3 shard_map.79
  6.4 5.0 %collective-permute-start.4 = (bf16[144,128]{1,0:T(8,128)(2,1)S(1)}, bf16[144,128]{1,0:T(8,128)(2,1)S(1)}, u32[]{:S(2)}, u32[]{:S(2)}) collective-permute-start(bf16[144,128]{1,0:T(8,128)(2,1)S(1)} %get-tuple-element.38), channel_id=1, source_target_pairs={{0,12},{4,8},{8,4},{12,0},{1,13},{5,9},{9,5},{13,1},{2,14},{6,10},... | collective-permute-start | bytes 110600 | tf_op jit(solution)/shard_map/ppermute | solution.py:253
  11.4 0.0 collective-permute-start.3
  11.4 0.6 %collective-permute-start.2 = (bf16[144,128]{1,0:T(8,128)(2,1)S(1)}, bf16[144,128]{1,0:T(8,128)(2,1)S(1)}, u32[]{:S(2)}, u32[]{:S(2)}) collective-permute-start(bf16[144,128]{1,0:T(8,128)(2,1)S(1)} %get-tuple-element.38), channel_id=1, source_target_pairs={{0,4},{4,0},{8,12},{12,8},{1,5},{5,1},{9,13},{13,9},{2,6},{6,2},{1... | collective-permute-start | bytes 110600 | tf_op jit(solution)/shard_map/ppermute | solution.py:253
  12.1 0.0 collective-permute-done.swapped_ref
  12.1 0.0 copy-done.1
  12.1 1.9 %shard_map.80 = (bf16[1536,128]{1,0:T(8,128)(2,1)S(1)}, f32[128,128]{1,0:T(8,128)S(1)}, bf16[128,128]{1,0:T(8,128)(2,1)S(1)}, f32[128,128]{1,0:T(8,128)S(1)}) custom-call(bf16[768,1536]{1,0:T(8,128)(2,1)S(1)} %bitcast.8, bf16[768,1536]{1,0:T(8,128)(2,1)S(1)} %collective-permute-done.swapped_ref, bf16[1536,128]{1,0:T(8,128)(2,1)S(1)} %bitcast.13, ...), custom_call_target="tpu_custom_call" | custom-call | tf_op jit(solution)/shard_map/pallas_call | solution.py:25
  14.0 0.0 collective-permute-done.4.refs_2_
  14.0 2.3 %collective-permute-done.3.refs_1_ = bf16[144,128]{1,0:T(8,128)(2,1)S(1)} collective-permute-done((bf16[144,128]{1,0:T(8,128)(2,1)S(1)}, bf16[144,128]{1,0:T(8,128)(2,1)S(1)}, u32[]{:S(2)}, u32[]{:S(2)}) %collective-permute-start.3) | collective-permute-done | bytes 36896 | tf_op jit(solution)/shard_map/ppermute | solution.py:253
  16.3 0.0 collective-permute-done.2.refs_0_
  16.3 0.4 %shard_map.81 = (bf16[128,384]{1,0:T(8,128)(2,1)S(1)}, f32[128,128]{1,0:T(8,128)S(1)}, f32[128,128]{1,0:T(8,128)S(1)}, bf16[128,128]{1,0:T(8,128)(2,1)S(1)}, bf1...) custom-call(bf16[144,128]{1,0:T(8,128)(2,1)S(1)} %collective-permute, ...), custom_call_target="tpu_custom_call" | custom-call | tf_op jit(solution)/shard_map/pallas_call | solution.py:25
  16.7 1.7 %collective-permute-start.7 = (bf16[128,128]{1,0:T(8,128)(2,1)S(1)}, bf16[128,128]{1,0:T(8,128)(2,1)S(1)}, u32[]{:S(2)}, u32[]{:S(2)}) collective-permute-start(bf16[128,128]{1,0:T(8,128)(2,1)S(1)} %get-tuple-element.47), channel_id=1, source_target_pairs={{0,12},{4,8},{8,4},{12,0},{1,13},{5,9},{9,5},{13,1},{2,14},{6,10},... | collective-permute-start | bytes 98312 | tf_op jit(solution)/shard_map/ppermute | solution.py:253
  18.4 0.5 %collective-permute-start.6 = (bf16[128,128]{1,0:T(8,128)(2,1)S(1)}, bf16[128,128]{1,0:T(8,128)(2,1)S(1)}, u32[]{:S(2)}, u32[]{:S(2)}) collective-permute-start(bf16[128,128]{1,0:T(8,128)(2,1)S(1)} %get-tuple-element.47), channel_id=1, source_target_pairs={{0,8},{4,12},{8,0},{12,4},{1,9},{5,13},{9,1},{13,5},{2,10},{6,14},... | collective-permute-start | bytes 98312 | tf_op jit(solution)/shard_map/ppermute | solution.py:253
  18.9 2.3 %collective-permute-start.5 = (bf16[128,128]{1,0:T(8,128)(2,1)S(1)}, bf16[128,128]{1,0:T(8,128)(2,1)S(1)}, u32[]{:S(2)}, u32[]{:S(2)}) collective-permute-start(bf16[128,128]{1,0:T(8,128)(2,1)S(1)} %get-tuple-element.47), channel_id=1, source_target_pairs={{0,4},{4,0},{8,12},{12,8},{1,5},{5,1},{9,13},{13,9},{2,6},{6,2},{1... | collective-permute-start | bytes 98312 | tf_op jit(solution)/shard_map/ppermute | solution.py:253
  21.1 1.9 %shard_map.82 = (bf16[1536,128]{1,0:T(8,128)(2,1)S(1)}, f32[128,128]{1,0:T(8,128)S(1)}, f32[128,128]{1,0:T(8,128)S(1)}) custom-call(bf16[768,1536]{1,0:T(8,128)(2,1)S(1)} %bitcast.9, bf16[768,1536]{1,0:T(8,128)(2,1)S(1)} %collective-permute-done.swapped_ref, bf16[1536,128]{1,0:T(8,128)(2,1)S(1)} %bitcast.14, f32[1536,128]{1,0:T(8,128)S(1)} %get-tuple-element.35.bound_ref, ...), custom_call_target="tpu_custom_call" | custom-call | tf_op jit(solution)/shard_map/pallas_call | solution.py:25
  23.0 0.0 collective-permute-done.7.refs_2_
  23.1 0.3 collective-permute-done.6.refs_1_
  23.3 0.1 collective-permute-done.5.refs_0_
  23.4 1.0 %shard_map.83 = (f32[128,128]{1,0:T(8,128)S(1)}, bf16[128,128]{1,0:T(8,128)(2,1)S(1)}, bf16[128,128]{1,0:T(8,128)(2,1)S(1)}, f32[128,128]{1,0:T(8,128)S(1)}, f32...) custom-call(bf16[128,128]{1,0:T(8,128)(2,1)S(1)} %collective-permute-done.5.refs_0_, ...), custom_call_target="tpu_custom_call" | custom-call | tf_op jit(solution)/shard_map/pallas_call | solution.py:25
  24.4 2.4 %collective-permute-start.10 = (bf16[128,128]{1,0:T(8,128)(2,1)S(1)}, bf16[128,128]{1,0:T(8,128)(2,1)S(1)}, u32[]{:S(2)}, u32[]{:S(2)}) collective-permute-start(bf16[128,128]{1,0:T(8,128)(2,1)S(1)} %get-tuple-element.63), channel_id=1, source_target_pairs={{0,12},{4,8},{8,4},{12,0},{1,13},{5,9},{9,5},{13,1},{2,14},{6,10},... | collective-permute-start | bytes 98312 | tf_op jit(solution)/shard_map/ppermute | solution.py:253
  26.7 0.8 %collective-permute-start.9 = (bf16[128,128]{1,0:T(8,128)(2,1)S(1)}, bf16[128,128]{1,0:T(8,128)(2,1)S(1)}, u32[]{:S(2)}, u32[]{:S(2)}) collective-permute-start(bf16[128,128]{1,0:T(8,128)(2,1)S(1)} %get-tuple-element.63), channel_id=1, source_target_pairs={{0,8},{4,12},{8,0},{12,4},{1,9},{5,13},{9,1},{13,5},{2,10},{6,14},... | collective-permute-start | bytes 98312 | tf_op jit(solution)/shard_map/ppermute | solution.py:253
  27.5 1.3 %collective-permute-start.8 = (bf16[128,128]{1,0:T(8,128)(2,1)S(1)}, bf16[128,128]{1,0:T(8,128)(2,1)S(1)}, u32[]{:S(2)}, u32[]{:S(2)}) collective-permute-start(bf16[128,128]{1,0:T(8,128)(2,1)S(1)} %get-tuple-element.63), channel_id=1, source_target_pairs={{0,4},{4,0},{8,12},{12,8},{1,5},{5,1},{9,13},{13,9},{2,6},{6,2},{1... | collective-permute-start | bytes 98312 | tf_op jit(solution)/shard_map/ppermute | solution.py:253
  28.7 1.7 %shard_map.84 = (f32[1536,128]{1,0:T(8,128)S(1)}, f32[128,128]{1,0:T(8,128)S(1)}) custom-call(bf16[768,1536]{1,0:T(8,128)(2,1)S(1)} %bitcast.10, bf16[768,1536]{1,0:T(8,128)(2,1)S(1)} %collective-permute-done.swapped_ref, f32[1536,128]{1,0:T(8,128)S(1)} %get-tuple-element.35.bound_ref, bf16[1536,128]{1,0:T(8,128)(2,1)S(1)} %get-tuple-element.36.place_ref, ...), custom_call_target="tpu_custom_call" | custom-call | tf_op jit(solution)/shard_map/pallas_call | solution.py:25
  30.5 0.9 %copy.8 = f32[1,1536,128]{2,1,0:T(8,128)} copy(f32[1,1536,128]{2,1,0:T(8,128)S(1)} %bitcast.4) | data formatting | bytes 1572864
  31.4 0.0 collective-permute-done.10.refs_2_
  31.4 0.3 collective-permute-done.9.refs_1_
  31.6 0.1 collective-permute-done.8.refs_0_
  31.8 0.2 shard_map.85
  31.9 0.6 %copy.9 = f32[1,128,128]{2,1,0:T(8,128)} copy(f32[1,128,128]{2,1,0:T(8,128)S(1)} %bitcast.5) | data formatting | bytes 131072
Async XLA Ops:
  0.6 5.5 %copy-start.4 = (s32[1,128]{1,0:T(1,128)S(1)}, s32[1,128]{1,0:T(1,128)}, u32[]{:S(2)}) copy-start(s32[1,128]{1,0:T(1,128)} %key_ref.7) | copy-start | bytes 1540
  0.6 5.5 %copy-start.3 = (s32[1,128]{1,0:T(1,128)S(1)}, s32[1,128]{1,0:T(1,128)}, u32[]{:S(2)}) copy-start(s32[1,128]{1,0:T(1,128)} %dest_ref.7) | copy-start | bytes 1540
  0.7 11.4 %collective-permute-start = (bf16[768,1536]{1,0:T(8,128)(2,1)}, bf16[768,1536]{1,0:T(8,128)(2,1)S(1)}, u32[]{:S(2)}, u32[]{:S(2)}) collective-permute-start(bf16[768,1536]{1,0:T(8,128)(2,1)} %bitcast.6), channel_id=1, source_target_pairs={{0,1},{1,0},{2,3},{3,2},{4,5},{5,4},{6,7},{7,6},{8,9},{9,8},{10,11... | collective-permute-start | bytes 7077896 | tf_op jit(solution)/shard_map/ppermute | solution.py:247
  1.2 1.7 %copy-start = (bf16[1,768,1536]{2,1,0:T(8,128)(2,1)S(1)}, bf16[1,768,1536]{2,1,0:T(8,128)(2,1)}, u32[]{:S(2)}) copy-start(bf16[1,768,1536]{2,1,0:T(8,128)(2,1)} %param.8) | copy-start | bytes 7077892
  2.9 0.7 %copy-start.6 = (s32[1,128]{1,0:T(1,128)S(1)}, s32[1,128]{1,0:T(1,128)}, u32[]{:S(2)}) copy-start(s32[1,128]{1,0:T(1,128)} %local_ref.3) | copy-start | bytes 1540
  3.5 1.0 %copy-start.2 = (bf16[1,1536,128]{2,1,0:T(8,128)(2,1)S(1)}, bf16[1,1536,128]{2,1,0:T(8,128)(2,1)}, u32[]{:S(2)}) copy-start(bf16[1,1536,128]{2,1,0:T(8,128)(2,1)} %param.9) | copy-start | bytes 1179652
  3.5 8.6 %copy-start.1 = (bf16[1,768,1536]{2,1,0:T(8,128)(2,1)S(1)}, bf16[1,768,1536]{2,1,0:T(8,128)(2,1)}, u32[]{:S(2)}) copy-start(bf16[1,768,1536]{2,1,0:T(8,128)(2,1)} %param.8) | copy-start | bytes 7077892
  4.1 2.1 %collective-permute-start.1 = (bf16[128,1536]{1,0:T(8,128)(2,1)S(1)}, bf16[128,1536]{1,0:T(8,128)(2,1)S(1)}, u32[]{:S(2)}, u32[]{:S(2)}) collective-permute-start(bf16[128,1536]{1,0:T(8,128)(2,1)S(1)} %shard_map.78.part_ref), channel_id=1, source_target_pairs={{0,1},{1,0},{2,3},{3,2},{4,5},{5,4},{6,7},{7,6},{8,9},{9,8},{10,11... | collective-permute-start | bytes 1179656 | tf_op jit(solution)/shard_map/ppermute | solution.py:247
  4.5 0.7 %copy-start.5 = (f32[1,1536]{1,0:T(1,128)S(1)}, f32[1,1536]{1,0:T(1,128)}, u32[]{:S(2)}) copy-start(f32[1,1536]{1,0:T(1,128)} %limit_ref.1) | copy-start | bytes 18436
  6.4 7.5 %collective-permute-start.4 = (bf16[144,128]{1,0:T(8,128)(2,1)S(1)}, bf16[144,128]{1,0:T(8,128)(2,1)S(1)}, u32[]{:S(2)}, u32[]{:S(2)}) collective-permute-start(bf16[144,128]{1,0:T(8,128)(2,1)S(1)} %get-tuple-element.38), channel_id=1, source_target_pairs={{0,12},{4,8},{8,4},{12,0},{1,13},{5,9},{9,5},{13,1},{2,14},{6,10},... | collective-permute-start | bytes 110600 | tf_op jit(solution)/shard_map/ppermute | solution.py:253
  11.4 4.9 %collective-permute-start.3 = (bf16[144,128]{1,0:T(8,128)(2,1)S(1)}, bf16[144,128]{1,0:T(8,128)(2,1)S(1)}, u32[]{:S(2)}, u32[]{:S(2)}) collective-permute-start(bf16[144,128]{1,0:T(8,128)(2,1)S(1)} %get-tuple-element.38), channel_id=1, source_target_pairs={{0,8},{4,12},{8,0},{12,4},{1,9},{5,13},{9,1},{13,5},{2,10},{6,14},... | collective-permute-start | bytes 110600 | tf_op jit(solution)/shard_map/ppermute | solution.py:253
  11.4 4.9 %collective-permute-start.2 = (bf16[144,128]{1,0:T(8,128)(2,1)S(1)}, bf16[144,128]{1,0:T(8,128)(2,1)S(1)}, u32[]{:S(2)}, u32[]{:S(2)}) collective-permute-start(bf16[144,128]{1,0:T(8,128)(2,1)S(1)} %get-tuple-element.38), channel_id=1, source_target_pairs={{0,4},{4,0},{8,12},{12,8},{1,5},{5,1},{9,13},{13,9},{2,6},{6,2},{1... | collective-permute-start | bytes 110600 | tf_op jit(solution)/shard_map/ppermute | solution.py:253
  16.7 6.4 %collective-permute-start.7 = (bf16[128,128]{1,0:T(8,128)(2,1)S(1)}, bf16[128,128]{1,0:T(8,128)(2,1)S(1)}, u32[]{:S(2)}, u32[]{:S(2)}) collective-permute-start(bf16[128,128]{1,0:T(8,128)(2,1)S(1)} %get-tuple-element.47), channel_id=1, source_target_pairs={{0,12},{4,8},{8,4},{12,0},{1,13},{5,9},{9,5},{13,1},{2,14},{6,10},... | collective-permute-start | bytes 98312 | tf_op jit(solution)/shard_map/ppermute | solution.py:253
  18.4 4.9 %collective-permute-start.6 = (bf16[128,128]{1,0:T(8,128)(2,1)S(1)}, bf16[128,128]{1,0:T(8,128)(2,1)S(1)}, u32[]{:S(2)}, u32[]{:S(2)}) collective-permute-start(bf16[128,128]{1,0:T(8,128)(2,1)S(1)} %get-tuple-element.47), channel_id=1, source_target_pairs={{0,8},{4,12},{8,0},{12,4},{1,9},{5,13},{9,1},{13,5},{2,10},{6,14},... | collective-permute-start | bytes 98312 | tf_op jit(solution)/shard_map/ppermute | solution.py:253
  18.9 4.5 %collective-permute-start.5 = (bf16[128,128]{1,0:T(8,128)(2,1)S(1)}, bf16[128,128]{1,0:T(8,128)(2,1)S(1)}, u32[]{:S(2)}, u32[]{:S(2)}) collective-permute-start(bf16[128,128]{1,0:T(8,128)(2,1)S(1)} %get-tuple-element.47), channel_id=1, source_target_pairs={{0,4},{4,0},{8,12},{12,8},{1,5},{5,1},{9,13},{13,9},{2,6},{6,2},{1... | collective-permute-start | bytes 98312 | tf_op jit(solution)/shard_map/ppermute | solution.py:253
  24.4 7.0 %collective-permute-start.10 = (bf16[128,128]{1,0:T(8,128)(2,1)S(1)}, bf16[128,128]{1,0:T(8,128)(2,1)S(1)}, u32[]{:S(2)}, u32[]{:S(2)}) collective-permute-start(bf16[128,128]{1,0:T(8,128)(2,1)S(1)} %get-tuple-element.63), channel_id=1, source_target_pairs={{0,12},{4,8},{8,4},{12,0},{1,13},{5,9},{9,5},{13,1},{2,14},{6,10},... | collective-permute-start | bytes 98312 | tf_op jit(solution)/shard_map/ppermute | solution.py:253
  26.7 4.9 %collective-permute-start.9 = (bf16[128,128]{1,0:T(8,128)(2,1)S(1)}, bf16[128,128]{1,0:T(8,128)(2,1)S(1)}, u32[]{:S(2)}, u32[]{:S(2)}) collective-permute-start(bf16[128,128]{1,0:T(8,128)(2,1)S(1)} %get-tuple-element.63), channel_id=1, source_target_pairs={{0,8},{4,12},{8,0},{12,4},{1,9},{5,13},{9,1},{13,5},{2,10},{6,14},... | collective-permute-start | bytes 98312 | tf_op jit(solution)/shard_map/ppermute | solution.py:253
  27.5 4.3 %collective-permute-start.8 = (bf16[128,128]{1,0:T(8,128)(2,1)S(1)}, bf16[128,128]{1,0:T(8,128)(2,1)S(1)}, u32[]{:S(2)}, u32[]{:S(2)}) collective-permute-start(bf16[128,128]{1,0:T(8,128)(2,1)S(1)} %get-tuple-element.63), channel_id=1, source_target_pairs={{0,4},{4,0},{8,12},{12,8},{1,5},{5,1},{9,13},{13,9},{2,6},{6,2},{1... | collective-permute-start | bytes 98312 | tf_op jit(solution)/shard_map/ppermute | solution.py:253
